TPU v7x, 512 devices: a whole 4x4x16 slice. The times are simulated.
512 devices in a mesh: rep: 2 (over x_hi), row: 8 (over y, x_lo), col: 32 (over z, core).
Axes of the slice: x: 4 (x_hi: 2, x_lo: 2; x = x_hi * 2 + x_lo), y: 4, z: 16, core: 2. Of those that a mesh axis runs over, the one named last changes fastest.
Arguments:
- tokens: bfloat16 [2, 32, 256, 2048], P('rep', 'col', None, 'row'), may hold values from -6 to 6
- w_qkv: bfloat16 [2048, 3, 2048], P('col', None, 'row'), may hold values from -0.125 to 0.125
- w_out: bfloat16 [2048, 2048], P('row', 'col'), may hold values from -0.125 to 0.125
- w_up: bfloat16 [2048, 8192], P('col', 'row'), may hold values from -0.125 to 0.125
- w_down: bfloat16 [8192, 2048], P('row', 'col'), may hold values from -0.0625 to 0.0625
- ln1_gain: float32 [2048], replicated, may hold values from 0.25 to 1.75
- ln2_gain: float32 [2048], replicated, may hold values from 0.25 to 1.75
- kv_pool: bfloat16 [2, 2, 256, 128, 2048], P('rep', None, 'col', None, 'row'), may hold values from -240 to 240
- page_table: int32 [2, 32, 8], P(None, 'col'), may hold values from 0 to 7, as said below
- lengths: int32 [2, 32], P(None, 'col'), may hold values from 1 to 1024, as said below
- moved: int32 [32], P('col'), may hold values 0 or 1
Outputs:
- layer_out: bfloat16 [2, 32, 256, 2048], P('rep', 'col', None, 'row')
Inputs may be any that keep to these rules, and one draw needn't show every extreme that they name: `page_table`: within each block of 1 slots of one replica, the page entries are a permutation of 0 to 7. `lengths`: some slot's cache holds the full 8 * 128 tokens.
All inputs are finite; a program needn't handle non-finite values. No bound on the sum of `moved` on one device may be relied on, other than what follows from the above.
Results may differ from a plain program's by a relative error of at most 0.019.
Values may be sent and summed in bfloat16 or wider, within the bound.
No kernel may reach another device: no remote copies, remote signals or barrier semaphores. Data moves between devices by JAX's collectives and lax.ppermute only.
A program may use at most 64 MiB of HBM per device.

v0:
```python
import jax
import jax.numpy as jnp
from jax import lax
from jax.sharding import PartitionSpec as P

D = 2048
H = 16


def swapped(value, axis, apart):
    return lax.ppermute(value, axis, [(i, i ^ 1 << apart) for i in range(lax.axis_size(axis))])


def normalize(values, gain):
    mean = jnp.mean(values, axis=-1, keepdims=True)
    centred = values - mean
    spread = jnp.mean(centred * centred, axis=-1, keepdims=True)
    return centred * lax.rsqrt(spread + 1e-05) * gain


def attend(query, new_keys, new_values, cache_keys, cache_values, length, slopes):
    seq = query.shape[0]
    heads = query.shape[1]
    head_width = query.shape[2]
    cache_len = cache_keys.shape[0]
    keys = jnp.concatenate([cache_keys, new_keys], axis=0).reshape(-1, heads, head_width)
    values = jnp.concatenate([cache_values, new_values], axis=0).reshape(-1, heads, head_width)
    scores = jnp.einsum("shd,khd->hsk", query, keys, preferred_element_type=jnp.float32)
    scores = scores * (1.0 / jnp.sqrt(jnp.float32(head_width)))
    steps = jnp.arange(seq, dtype=jnp.int32)
    cache_pos = jnp.arange(cache_len, dtype=jnp.int32)
    query_pos = length + steps
    key_pos = jnp.concatenate([cache_pos, length + steps])
    cache_ok = jnp.broadcast_to((cache_pos < length)[None, :], (seq, cache_len))
    new_ok = steps[None, :] <= steps[:, None]
    allowed = jnp.concatenate([cache_ok, new_ok], axis=1)
    distance = (query_pos[:, None] - key_pos[None, :]).astype(jnp.float32)
    scores = scores - slopes[:, None, None] * distance[None, :, :]
    masked = jnp.where(allowed[None], scores, -1e30)
    top = jnp.max(masked, axis=-1, keepdims=True)
    weights = jnp.where(allowed[None], jnp.exp(masked - top), 0.0)
    total = jnp.sum(weights, axis=-1)
    summed = jnp.einsum(
        "hsk,khd->shd", weights.astype(jnp.bfloat16), values, preferred_element_type=jnp.float32
    )
    result = summed / jnp.transpose(total)[:, :, None]
    return result.reshape(seq, heads * head_width).astype(jnp.bfloat16)


def local(
    tokens, w_qkv, w_out, w_up, w_down, ln1_gain, ln2_gain, kv_pool, page_table, lengths, moved
):
    rep_index = lax.axis_index("rep")
    row_index = lax.axis_index("row")
    whole = lax.all_gather(tokens, "row", axis=3, tiled=True)
    per_dev = whole.shape[1]
    seq = whole.shape[2]
    width = whole.shape[3]
    share = tokens.shape[3]
    head_width = D // H
    heads = share // head_width
    rows = whole.reshape(per_dev * seq, width)
    normed = normalize(rows.astype(jnp.float32), ln1_gain).astype(jnp.bfloat16)
    piece = lax.all_gather(w_qkv, "col", axis=0, tiled=True)
    columns = normed
    qkv = jnp.dot(columns, piece.reshape(piece.shape[0], -1), preferred_element_type=jnp.float32)
    qkv = qkv.astype(jnp.bfloat16).reshape(per_dev, seq, 3, share)
    head_ids = (row_index * heads + jnp.arange(heads, dtype=jnp.int32) + 1).astype(jnp.float32)
    slopes = 2.0 ** (-8.0 * head_ids / H)
    store_keys = kv_pool[0, 0]
    store_values = kv_pool[0, 1]

    def pages_of(store, table):
        return store[table].reshape(-1, store.shape[2])

    other = swapped(kv_pool, "rep", 0)
    flag = moved[0] == 1
    home = jnp.where(flag, 1 - rep_index, rep_index)
    table = page_table[home, 0]
    length = lengths[home, 0]
    cache_keys = jnp.where(flag, pages_of(other[0, 0], table), pages_of(store_keys, table))
    cache_values = jnp.where(flag, pages_of(other[0, 1], table), pages_of(store_values, table))
    job = qkv[0]
    query = job[:, 0].reshape(seq, heads, head_width)
    results = [attend(query, job[:, 1], job[:, 2], cache_keys, cache_values, length, slopes)]
    attn = jnp.stack(results)
    attn_rows = attn.reshape(per_dev * seq, share)
    partial_mix = jnp.dot(
        attn_rows,
        lax.all_gather(w_out, "col", axis=1, tiled=True),
        preferred_element_type=jnp.float32,
    )
    local_inputs = tokens.reshape(per_dev * seq, share).astype(jnp.float32)
    mixed = lax.psum_scatter(
        partial_mix.astype(jnp.bfloat16), "row", scatter_dimension=1, tiled=True
    ).astype(jnp.float32)
    state_local = (local_inputs + mixed).astype(jnp.bfloat16)
    state = lax.all_gather(state_local, "row", axis=1, tiled=True)
    normed2 = normalize(state.astype(jnp.float32), ln2_gain).astype(jnp.bfloat16)
    columns = normed2
    hidden = jax.nn.gelu(
        jnp.dot(
            columns,
            lax.all_gather(w_up, "col", axis=0, tiled=True),
            preferred_element_type=jnp.float32,
        ),
        approximate=True,
    ).astype(jnp.bfloat16)
    partial_down = jnp.dot(
        hidden,
        lax.all_gather(w_down, "col", axis=1, tiled=True),
        preferred_element_type=jnp.float32,
    )
    down = lax.psum_scatter(
        partial_down.astype(jnp.bfloat16), "row", scatter_dimension=1, tiled=True
    ).astype(jnp.float32)
    finished = (state_local.astype(jnp.float32) + down).astype(jnp.bfloat16)
    return finished.reshape(tokens.shape)


def solution(mesh):
    return jax.shard_map(
        local,
        mesh=mesh,
        in_specs=(
            P("rep", "col", None, "row"),
            P("col", None, "row"),
            P("row", "col"),
            P("col", "row"),
            P("row", "col"),
            P(),
            P(),
            P("rep", None, "col", None, "row"),
            P(None, "col", None),
            P(None, "col"),
            P("col"),
        ),
        out_specs=P("rep", "col", None, "row"),
        check_vma=False,
    )
```

profile of v0, /device:TPU:1, one launch (start us, length us, event | category | flops | bytes accessed | tf_op | source)
XLA Modules:
  0.0 516.2 jit_solution(1419734177115144409)
XLA Ops:
  6.5 0.7 all-gather.7.cloned.1.call-update
  7.3 0.7 all-gather.9.cloned.1.call-update
  8.1 5.5 %collective-permute-start = (bf16[1,2,8,128,256]{4,3,2,1,0:T(8,128)(2,1)}, bf16[1,2,8,128,256]{4,3,2,1,0:T(8,128)(2,1)}, u32[]{:S(2)}, u32[]{:S(2)}) collective-permute-start(bf16[1,2,8,128,256]{4,3,2,1,0:T(8,128)(2,1)} %param.18), channel_id=1, source_target_pairs={{0,256},{256,0},{1,257},{257,1},{2,258},{258,2},{3,259},{259,3},{4... | collective-permute-start | bytes 3145736 | tf_op jit(solution)/shard_map/ppermute | solution.py:11
  13.6 1.3 slice_bitcast_fusion.2
  15.6 0.6 constant_dynamic-slice_fusion
  16.2 0.6 iota_add_fusion
  16.7 0.6 iota_compare_fusion.1
  17.4 0.7 fusion.62
  18.0 0.6 gather_fusion.1
  18.6 0.6 gather_fusion.3
  19.3 0.9 pad_add_fusion
  20.1 0.2 subtract_convert_fusion
  20.3 14.5 %collective-permute-done = bf16[1,2,8,128,256]{4,3,2,1,0:T(8,128)(2,1)} collective-permute-done((bf16[1,2,8,128,256]{4,3,2,1,0:T(8,128)(2,1)}, bf16[1,2,8,128,256]{4,3,2,1,0:T(8,128)(2,1)}, u32[]{:S(2)}, u32[]{:S(2)}) %collective-permute-start) | collective-permute-done | bytes 1048608 | tf_op jit(solution)/shard_map/ppermute | solution.py:11
  34.8 1.3 slice_bitcast_fusion
  36.1 1.4 gather_fusion
  37.5 1.4 gather_fusion.2
  38.9 0.2 broadcast_select_fusion
  39.1 0.1 reshape.194
  39.2 0.1 copy.25
  39.3 0.1 reshape.193
  39.4 1.2 copy.29
  40.6 21.2 %all-gather.7.cloned.1.call-done = bf16[1,1,256,2048]{3,2,1,0:T(8,128)(2,1)} async-done(((bf16[1,1,256,256]{3,2,1,0:T(8,128)(2,1)}), bf16[1,1,256,2048]{3,2,1,0:T(8,128)(2,1)}) %all-gather.7.cloned.1.call-update) | async-done | bytes 1048592 | tf_op jit(solution)/shard_map/all_gather | solution.py:55
  61.7 1.4 convert_reduce_fusion
  63.2 1.6 fusion.16
  64.9 77.3 %all-gather.9.cloned.1.call-done = bf16[2048,3,256]{2,0,1:T(8,128)(2,1)} async-done(((bf16[64,3,256]{2,0,1:T(8,128)(2,1)}), bf16[2048,3,256]{2,0,1:T(8,128)(2,1)}) %all-gather.9.cloned.1.call-update) | async-done | bytes 3145744 | tf_op jit(solution)/shard_map/all_gather | solution.py:64
  142.2 4.7 copy.22
  146.9 3.8 convolution_convert_fusion.2
  150.7 1.2 copy.23
  151.9 0.1 copy.26
  152.0 0.9 fusion.3
  152.9 1.5 copy-done.2
  154.4 0.9 fusion.72
  155.3 0.2 copy-done.6
  155.5 3.3 fusion.25
  158.8 53.2 %all-gather.11.cloned.1.call-done = bf16[256,2048]{0,1:T(8,128)(2,1)} async-done(((bf16[256,64]{0,1:T(8,128)(2,1)}), bf16[256,2048]{0,1:T(8,128)(2,1)}) %all-gather.11.cloned.1.call-update) | async-done | bytes 1048592 | tf_op jit(solution)/shard_map/all_gather | solution.py:90
  212.1 2.7 convolution_convert_fusion.1
  214.8 41.0 %reduce-scatter.3.cloned.1.call-done = bf16[256,256]{1,0:T(8,128)(2,1)} async-done(((bf16[256,2048]{1,0:T(8,128)(2,1)}), bf16[256,256]{1,0:T(8,128)(2,1)}) %reduce-scatter.3.cloned.1.call-update) | async-done | bytes 131088 | tf_op jit(solution)/shard_map/reduce_scatter | solution.py:94
  255.9 1.6 fusion.60
  257.5 0.5 all-gather.15.cloned.1.call-update
  258.1 0.7 all-gather.17.cloned.1.call-update
  258.9 45.7 %all-gather.13.cloned.1.call-done = bf16[256,2048]{1,0:T(8,128)(2,1)} async-done(((bf16[256,256]{1,0:T(8,128)(2,1)}), bf16[256,2048]{1,0:T(8,128)(2,1)}) %all-gather.13.cloned.1.call-update) | async-done | bytes 1048592 | tf_op jit(solution)/shard_map/all_gather | solution.py:98
  304.6 1.4 convert_reduce_fusion.1
  306.0 1.6 fusion.8
  307.7 78.6 %all-gather.15.cloned.1.call-done = bf16[2048,1024]{1,0:T(8,128)(2,1)} async-done(((bf16[64,1024]{1,0:T(8,128)(2,1)}), bf16[2048,1024]{1,0:T(8,128)(2,1)}) %all-gather.15.cloned.1.call-update) | async-done | bytes 4194320 | tf_op jit(solution)/shard_map/all_gather | solution.py:104
  386.3 73.0 %all-gather.17.cloned.1.call-done = bf16[1024,2048]{0,1:T(8,128)(2,1)} async-done(((bf16[1024,64]{0,1:T(8,128)(2,1)}), bf16[1024,2048]{0,1:T(8,128)(2,1)}) %all-gather.17.cloned.1.call-update) | async-done | bytes 4194320 | tf_op jit(solution)/shard_map/all_gather | solution.py:111
  459.3 7.5 %convolution_convert_fusion = bf16[256,2048]{1,0:T(8,128)(2,1)} fusion(bf16[1024,2048]{0,1:T(8,128)(2,1)} %all-gather.17.cloned.1.call-done, bf16[2048,1024]{1,0:T(8,128)(2,1)} %all-gather.15.cloned.1.call-done, bf16[256,2048]{1,0:T(8,128)(2,1)} %all-gather.13.cloned.1.call-done, f32[2048]{0:T(1024)S(1)} %copy-done.8, f32[256]{0:T(256)S(1)} %add_rsqrt_fusion, ...), kind=kOutput, calls=%fused_computation.16 | convolution fusion | flops 2152988672 | bytes 10496000 | tf_op jit(solution)/shard_map/dot_general | solution.py:109
  466.8 41.0 %reduce-scatter.5.cloned.1.call-done = bf16[256,256]{1,0:T(8,128)(2,1)} async-done(((bf16[256,2048]{1,0:T(8,128)(2,1)}), bf16[256,256]{1,0:T(8,128)(2,1)}) %reduce-scatter.5.cloned.1.call-update) | async-done | bytes 131088 | tf_op jit(solution)/shard_map/reduce_scatter | solution.py:114
  507.8 1.6 fusion.61
  (39 shorter events, 0.5 us)
Async XLA Ops:
  6.5 9.0 %copy-start = (s32[2,1]{0,1:T(1,128)S(1)}, s32[2,1]{0,1:T(1,128)}, u32[]{:S(2)}) copy-start(s32[2,1]{0,1:T(1,128)} %param.20) | copy-start | bytes 28
  6.5 55.2 %all-gather.7.cloned.1.call-start = ((), (), s32[]{:S(2)}) async-start(), calls=%async_computation.2 | async-start | bytes 1179648 | tf_op jit(solution)/shard_map/all_gather | solution.py:55
  7.3 134.9 %all-gather.9.cloned.1.call-start = ((), (), s32[]{:S(2)}) async-start(), calls=%async_computation.3 | async-start | bytes 3244032 | tf_op jit(solution)/shard_map/all_gather | solution.py:64
  8.0 204.1 %all-gather.11.cloned.1.call-start = ((), (), s32[]{:S(2)}) async-start(), calls=%async_computation.4 | async-start | bytes 1081344 | tf_op jit(solution)/shard_map/all_gather | solution.py:90
  8.1 26.8 %collective-permute-start = (bf16[1,2,8,128,256]{4,3,2,1,0:T(8,128)(2,1)}, bf16[1,2,8,128,256]{4,3,2,1,0:T(8,128)(2,1)}, u32[]{:S(2)}, u32[]{:S(2)}) collective-permute-start(bf16[1,2,8,128,256]{4,3,2,1,0:T(8,128)(2,1)} %param.18), channel_id=1, source_target_pairs={{0,256},{256,0},{1,257},{257,1},{2,258},{258,2},{3,259},{259,3},{4... | collective-permute-start | bytes 3145736 | tf_op jit(solution)/shard_map/ppermute | solution.py:11
  13.6 242.3 %reduce-scatter.3.cloned.1.call-start = ((), (), s32[]{:S(2)}) async-start(), calls=%async_computation.5 | async-start | bytes 1179648 | tf_op jit(solution)/shard_map/reduce_scatter | solution.py:94
  64.8 82.1 %copy-start.1 = (bf16[1,1,256,2048]{3,2,1,0:T(8,128)(2,1)S(1)}, bf16[1,1,256,2048]{3,2,1,0:T(8,128)(2,1)}, u32[]{:S(2)}) copy-start(bf16[1,1,256,2048]{3,2,1,0:T(8,128)(2,1)} %all-gather.7.cloned.1.call-done) | copy-start | bytes 3145732
  64.8 82.0 %copy-start.7 = (f32[2048]{0:T(1024)S(1)}, f32[2048]{0:T(1024)}, u32[]{:S(2)}) copy-start(f32[2048]{0:T(1024)} %param.16) | copy-start | bytes 24580
  146.9 5.1 copy-start.3
  152.9 1.5 copy-start.2
  154.4 1.0 copy-start.6
  158.8 97.0 %copy-start.5 = (bf16[1,1,256,256]{3,2,1,0:T(8,128)(2,1)S(1)}, bf16[1,1,256,256]{3,2,1,0:T(8,128)(2,1)}, u32[]{:S(2)}) copy-start(bf16[1,1,256,256]{3,2,1,0:T(8,128)(2,1)} %param.11) | copy-start | bytes 393220
  212.1 247.3 %copy-start.8 = (f32[2048]{0:T(1024)S(1)}, f32[2048]{0:T(1024)}, u32[]{:S(2)}) copy-start(f32[2048]{0:T(1024)} %param.17) | copy-start | bytes 24580
  214.8 89.8 %all-gather.13.cloned.1.call-start = ((), (), s32[]{:S(2)}) async-start(), calls=%async_computation.6 | async-start | bytes 1179648 | tf_op jit(solution)/shard_map/all_gather | solution.py:98
  257.5 128.8 %all-gather.15.cloned.1.call-start = ((), (), s32[]{:S(2)}) async-start(), calls=%async_computation.7 | async-start | bytes 4325376 | tf_op jit(solution)/shard_map/all_gather | solution.py:104
  258.1 201.3 %all-gather.17.cloned.1.call-start = ((), (), s32[]{:S(2)}) async-start(), calls=%async_computation.8 | async-start | bytes 4325376 | tf_op jit(solution)/shard_map/all_gather | solution.py:111
  258.8 249.0 %reduce-scatter.5.cloned.1.call-start = ((), (), s32[]{:S(2)}) async-start(), calls=%async_computation.9 | async-start | bytes 1179648 | tf_op jit(solution)/shard_map/reduce_scatter | solution.py:114
  307.7 200.1 %copy-start.4 = (bf16[256,256]{1,0:T(8,128)(2,1)S(1)}, bf16[256,256]{1,0:T(8,128)(2,1)}, u32[]{:S(2)}) copy-start(bf16[256,256]{1,0:T(8,128)(2,1)} %fusion.60) | copy-start | bytes 393220
Sparse Core Ops, SparseCore 0:
  9.4 52.3 all-gather.6
  63.9 78.2 all-gather.8
  144.3 67.7 all-gather.10
  214.9 40.8 reduce-scatter.2
  257.7 46.8 all-gather.12
  306.6 79.6 all-gather.14
  388.4 70.8 all-gather.16
  466.9 40.8 reduce-scatter.4
where the time goes:
time: 520 us; the launch traced here: 516 us
  waiting for transfers between devices  448 us (86%)
  matrix products  18.2 us (4%)
  local copies, waits for them, and re-layouts  16.3 us (3%)
  between operations  14.4 us (3%)
  other arithmetic  13.3 us (3%)
  starting transfers between devices  5.76 us (1%)
    all_gather x1, waiting for transfers between devices, local(): lax.all_gather(w_up, 'col', axis=0, tiled=True)  78.6 us
    all_gather x1, waiting for transfers between devices, local(): piece = lax.all_gather(w_qkv, 'col', axis=0, tiled=True)  77.3 us
    all_gather x1, waiting for transfers between devices, local(): lax.all_gather(w_down, 'col', axis=1, tiled=True)  73 us
    all_gather x1, waiting for transfers between devices, local(): lax.all_gather(w_out, 'col', axis=1, tiled=True)  53.2 us
    all_gather x1, waiting for transfers between devices, local(): state = lax.all_gather(state_local, 'row', axis=1, tiled=True)  45.7 us
    reduce_scatter x1, waiting for transfers between devices, local(): lax.psum_scatter(partial_mix.astype(jnp.bfloat16), 'row', scatter_dimensi...  41 us
    reduce_scatter x1, waiting for transfers between devices, local(): lax.psum_scatter(partial_down.astype(jnp.bfloat16), 'row', scatter_dimens...  41 us
    all_gather x1, waiting for transfers between devices, local(): whole = lax.all_gather(tokens, 'row', axis=3, tiled=True)  21.2 us
  transfers between devices with their start and end apart: 9, of which 9 were waited for; matrix products, arithmetic and copies ran while one was open for 6% of the time, Pallas kernels for 0%

commit v1 on v0

--- a/solution.py
+++ b/solution.py
@@ -47,73 +47,68 @@
     return result.reshape(seq, heads * head_width).astype(jnp.bfloat16)
 
 
+def row_gather(value):
+    copies = jnp.broadcast_to(value[None], (lax.axis_size("row"),) + value.shape)
+    parts = lax.all_to_all(copies, "row", 0, 0, tiled=True)
+    return jnp.swapaxes(parts, 0, 1).reshape(value.shape[0], -1)
+
+
+def row_scatter_sum(partial):
+    size = lax.axis_size("row")
+    parts = partial.reshape(partial.shape[0], size, -1)
+    parts = jnp.swapaxes(parts, 0, 1).astype(jnp.bfloat16)
+    parts = lax.all_to_all(parts, "row", 0, 0, tiled=True)
+    return jnp.sum(parts.astype(jnp.float32), axis=0)
+
+
+def times_transposed(left, right):
+    return lax.dot_general(left, right, (((1,), (1,)), ((), ())), preferred_element_type=jnp.float32)
+
+
 def local(
     tokens, w_qkv, w_out, w_up, w_down, ln1_gain, ln2_gain, kv_pool, page_table, lengths, moved
 ):
     rep_index = lax.axis_index("rep")
     row_index = lax.axis_index("row")
-    whole = lax.all_gather(tokens, "row", axis=3, tiled=True)
-    per_dev = whole.shape[1]
-    seq = whole.shape[2]
-    width = whole.shape[3]
+    seq = tokens.shape[2]
     share = tokens.shape[3]
+    hidden_share = w_up.shape[1]
     head_width = D // H
     heads = share // head_width
-    rows = whole.reshape(per_dev * seq, width)
+    shard = jnp.concatenate(
+        [w_qkv.reshape(w_qkv.shape[0], -1), w_out.T, w_up, w_down.T], axis=1
+    )
+    weights = lax.all_gather(shard, "col", axis=0, tiled=True)
+    cut = [0, 3 * share, 4 * share, 4 * share + hidden_share, 4 * share + 2 * hidden_share]
+    all_qkv, all_out, all_up, all_down = [weights[:, a:b] for a, b in zip(cut[:-1], cut[1:])]
+    other = swapped(kv_pool, "rep", 0)
+    inputs = tokens.reshape(seq, share)
+    rows = row_gather(inputs)
     normed = normalize(rows.astype(jnp.float32), ln1_gain).astype(jnp.bfloat16)
-    piece = lax.all_gather(w_qkv, "col", axis=0, tiled=True)
-    columns = normed
-    qkv = jnp.dot(columns, piece.reshape(piece.shape[0], -1), preferred_element_type=jnp.float32)
-    qkv = qkv.astype(jnp.bfloat16).reshape(per_dev, seq, 3, share)
     head_ids = (row_index * heads + jnp.arange(heads, dtype=jnp.int32) + 1).astype(jnp.float32)
     slopes = 2.0 ** (-8.0 * head_ids / H)
-    store_keys = kv_pool[0, 0]
-    store_values = kv_pool[0, 1]
 
     def pages_of(store, table):
         return store[table].reshape(-1, store.shape[2])
 
-    other = swapped(kv_pool, "rep", 0)
     flag = moved[0] == 1
     home = jnp.where(flag, 1 - rep_index, rep_index)
     table = page_table[home, 0]
     length = lengths[home, 0]
-    cache_keys = jnp.where(flag, pages_of(other[0, 0], table), pages_of(store_keys, table))
-    cache_values = jnp.where(flag, pages_of(other[0, 1], table), pages_of(store_values, table))
-    job = qkv[0]
-    query = job[:, 0].reshape(seq, heads, head_width)
-    results = [attend(query, job[:, 1], job[:, 2], cache_keys, cache_values, length, slopes)]
-    attn = jnp.stack(results)
-    attn_rows = attn.reshape(per_dev * seq, share)
-    partial_mix = jnp.dot(
-        attn_rows,
-        lax.all_gather(w_out, "col", axis=1, tiled=True),
-        preferred_element_type=jnp.float32,
-    )
-    local_inputs = tokens.reshape(per_dev * seq, share).astype(jnp.float32)
-    mixed = lax.psum_scatter(
-        partial_mix.astype(jnp.bfloat16), "row", scatter_dimension=1, tiled=True
-    ).astype(jnp.float32)
-    state_local = (local_inputs + mixed).astype(jnp.bfloat16)
-    state = lax.all_gather(state_local, "row", axis=1, tiled=True)
+    cache_keys = jnp.where(flag, pages_of(other[0, 0], table), pages_of(kv_pool[0, 0], table))
+    cache_values = jnp.where(flag, pages_of(other[0, 1], table), pages_of(kv_pool[0, 1], table))
+    qkv = jnp.dot(normed, all_qkv, preferred_element_type=jnp.float32)
+    qkv = qkv.astype(jnp.bfloat16).reshape(seq, 3, share)
+    query = qkv[:, 0].reshape(seq, heads, head_width)
+    attn = attend(query, qkv[:, 1], qkv[:, 2], cache_keys, cache_values, length, slopes)
+    mixed = row_scatter_sum(times_transposed(attn, all_out))
+    state_local = (inputs.astype(jnp.float32) + mixed).astype(jnp.bfloat16)
+    state = row_gather(state_local)
     normed2 = normalize(state.astype(jnp.float32), ln2_gain).astype(jnp.bfloat16)
-    columns = normed2
     hidden = jax.nn.gelu(
-        jnp.dot(
-            columns,
-            lax.all_gather(w_up, "col", axis=0, tiled=True),
-            preferred_element_type=jnp.float32,
-        ),
-        approximate=True,
+        jnp.dot(normed2, all_up, preferred_element_type=jnp.float32), approximate=True
     ).astype(jnp.bfloat16)
-    partial_down = jnp.dot(
-        hidden,
-        lax.all_gather(w_down, "col", axis=1, tiled=True),
-        preferred_element_type=jnp.float32,
-    )
-    down = lax.psum_scatter(
-        partial_down.astype(jnp.bfloat16), "row", scatter_dimension=1, tiled=True
-    ).astype(jnp.float32)
+    down = row_scatter_sum(times_transposed(hidden, all_down))
     finished = (state_local.astype(jnp.float32) + down).astype(jnp.bfloat16)
     return finished.reshape(tokens.shape)
 

time: 520 us -> 185 us (0.36)
  waiting for transfers between devices: 448 us -> 65.3 us
  blocking collectives: 0 us -> 53.1 us
    all_gather x6 -> x1, waiting for transfers between devices: 349 us -> 42 us  [local(): weights = lax.all_gather(shard, 'col', axis=0, tiled=True)]
    reduce_scatter x2 -> x0, waiting for transfers between devices: 82 us -> none  [the longest x1 41 us: local(): lax.psum_scatter(partial_mix.astype(jnp.bfloat16), 'row', scatter_dimensi...]
    all_to_all x0 -> x3, blocking collectives: none -> 53.1 us  [the longest x2 35.9 us: row_scatter_sum(): parts = lax.all_to_all(parts, 'row', 0, 0, tiled=True)]
    ppermute x1, waiting for transfers between devices: 14.5 us -> 23.3 us  [swapped(): lax.ppermute(value, axis, [(i, i ^ 1 << apart) for i in range(lax.axis_si...]
    all_to_all x0 -> x1, starting transfers between devices: none -> 5.95 us  [row_gather(): parts = lax.all_to_all(copies, 'row', 0, 0, tiled=True)]
  transfers between devices with their start and end apart: 9 -> 3, of which waited for: 9 -> 2; matrix products, arithmetic and copies ran while one was open for 6% -> 9% of each run, Pallas kernels for 0% -> 0%
where the time goes in v1:
time: 185 us; the launch traced here: 183 us
  waiting for transfers between devices  65.3 us (35%)
  blocking collectives  53.1 us (29%)
  local copies, waits for them, and re-layouts  15.1 us (8%)
  matrix products  14.7 us (8%)
  between operations  14.4 us (8%)
  other arithmetic  10.4 us (6%)
  starting transfers between devices  10.3 us (6%)
    all_gather x1, waiting for transfers between devices, local(): weights = lax.all_gather(shard, 'col', axis=0, tiled=True)  42 us
    all_to_all x2, blocking collectives, row_scatter_sum(): parts = lax.all_to_all(parts, 'row', 0, 0, tiled=True)  35.9 us
    ppermute x1, waiting for transfers between devices, swapped(): lax.ppermute(value, axis, [(i, i ^ 1 << apart) for i in range(lax.axis_si...  23.3 us
    all_to_all x1, blocking collectives, row_gather(): parts = lax.all_to_all(copies, 'row', 0, 0, tiled=True)  17.2 us
    dot_general x2, matrix products, times_transposed(): lax.dot_general(left, right, (((1,), (1,)), ((), ())), preferred_element_...  6.56 us
    all_to_all x1, starting transfers between devices, row_gather(): parts = lax.all_to_all(copies, 'row', 0, 0, tiled=True)  5.95 us
    gather x4, local copies, waits for them, and re-layouts, pages_of(): return store[table].reshape(-1, store.shape[2])  4.71 us
    ppermute x1, starting transfers between devices, swapped(): lax.ppermute(value, axis, [(i, i ^ 1 << apart) for i in range(lax.axis_si...  4.35 us
  transfers between devices with their start and end apart: 3, of which 2 were waited for; matrix products, arithmetic and copies ran while one was open for 9% of the time, Pallas kernels for 0%

profile of v1, /device:TPU:1, one launch (start us, length us, event | category | flops | bytes accessed | tf_op | source)
XLA Modules:
  0.0 183.2 jit_solution(10960020712580097508)
XLA Ops:
  6.5 0.9 copy.44
  7.5 1.8 pad_maximum_fusion
  9.2 1.0 copy.27
  10.2 1.1 broadcast_in_dim.23
  11.4 5.9 %all-to-all-start = ((bf16[8,256,256]{1,2,0:T(8,128)(2,1)}), bf16[8,256,256]{1,2,0:T(8,128)(2,1)S(1)}, u32[]{:S(2)}, u32[]{:S(2)}) async-start(bf16[8,256,256]{1,2,0:T(8,128)(2,1)} %broadcast_in_dim.23), calls=%async_computation | async-start | bytes 2097152 | tf_op jit(solution)/shard_map/all_to_all | solution.py:52
  17.3 4.3 %collective-permute-start = (bf16[1,2,8,128,256]{4,3,2,1,0:T(8,128)(2,1)}, bf16[1,2,8,128,256]{4,3,2,1,0:T(8,128)(2,1)}, u32[]{:S(2)}, u32[]{:S(2)}) collective-permute-start(bf16[1,2,8,128,256]{4,3,2,1,0:T(8,128)(2,1)} %param.18), channel_id=1, source_target_pairs={{0,256},{256,0},{1,257},{257,1},{2,258},{258,2},{3,259},{259,3},{4... | collective-permute-start | bytes 3145736 | tf_op jit(solution)/shard_map/ppermute | solution.py:11
  22.4 1.3 slice_bitcast_fusion.2
  23.6 0.6 gather_fusion.3
  24.2 1.4 gather_fusion.1
  25.6 0.6 constant_dynamic-slice_fusion
  26.2 0.6 iota_compare_fusion.1
  26.9 0.6 iota_add_fusion
  27.5 0.8 pad_add_fusion
  28.4 0.2 subtract_convert_fusion
  28.6 0.3 convert_reduce_fusion.3
  28.8 0.3 multiply_reduce_fusion.1
  29.2 1.4 fusion.20
  30.6 23.3 %collective-permute-done = bf16[1,2,8,128,256]{4,3,2,1,0:T(8,128)(2,1)} collective-permute-done((bf16[1,2,8,128,256]{4,3,2,1,0:T(8,128)(2,1)}, bf16[1,2,8,128,256]{4,3,2,1,0:T(8,128)(2,1)}, u32[]{:S(2)}, u32[]{:S(2)}) %collective-permute-start) | collective-permute-done | bytes 1048608 | tf_op jit(solution)/shard_map/ppermute | solution.py:11
  53.9 1.3 slice_bitcast_fusion
  55.2 1.4 gather_fusion.2
  56.6 1.4 gather_fusion
  58.0 1.5 broadcast_select_fusion
  59.4 0.1 reshape.203
  59.6 0.4 copy.39
  60.0 0.1 reshape.204
  60.1 0.1 copy.31
  60.2 42.0 %all-gather.2.cloned.1.call-done = bf16[2048,3072]{1,0:T(8,128)(2,1)} async-done(((bf16[64,3072]{1,0:T(8,128)(2,1)}), bf16[2048,3072]{1,0:T(8,128)(2,1)}) %all-gather.2.cloned.1.call-update) | async-done | bytes 12582928 | tf_op jit(solution)/shard_map/all_gather | solution.py:81
  102.2 4.0 %fusion.24 = bf16[256,768]{1,0:T(8,128)(2,1)} fusion(bf16[256,2048]{0,1:T(8,128)(2,1)} %fusion.20, bf16[2048,3072]{1,0:T(8,128)(2,1)} %all-gather.2.cloned.1.call-done), kind=kOutput, calls=%fused_computation.37 | convolution fusion | flops 805502976 | bytes 4587520 | tf_op jit(solution)/shard_map/dot_general | solution.py:100
  106.2 1.2 copy.29
  107.4 0.1 copy.32
  107.5 0.9 fusion.7
  108.4 0.9 fusion.72
  109.3 0.6 copy-done.1
  109.9 3.3 %fusion.33 = bf16[256,2,128]{0,2,1:T(8,128)(2,1)S(1)} fusion(bf16[256,2,128]{0,2,1:T(8,128)(2,1)S(1)} %bitcast.91, bf16[1024,2,128]{0,2,1:T(8,128)(2,1)S(1)} %copy.39, f32[256,2]{0,1:T(2,128)S(1)} %bitcast.94, f32[2,256,1280]{2,1,0:T(8,128)} %copy-done.1, pred[256,1280]{1,0:T(8,128)(4,1)S(1)} %copy-done.3), kind=kOutput, calls=%fused_computation.40 | convolution fusion | flops 171181824 | bytes 3737600 | tf_op jit(solution)/shard_map/hsk,khd->shd/dot_general | solution.py:43
  113.2 1.2 slice-done
  114.4 0.5 fusion.21
  114.9 19.8 %all_to_all.20 = bf16[8,256,256]{2,1,0:T(8,128)(2,1)S(1)} all-to-all(bf16[8,256,256]{2,1,0:T(8,128)(2,1)S(1)} %fusion.21), channel_id=1, replica_groups=mesh['rep'=2,'row'=8,'col'=32] {'row'}, dimensions={0} | all-to-all | bytes 2097152 | tf_op jit(solution)/shard_map/all_to_all | solution.py:60
  134.7 0.1 convert_reduce_fusion.1
  134.9 0.1 copy.35
  135.0 0.1 broadcast_in_dim.32
  135.1 17.2 %all_to_all.21 = bf16[8,256,256]{1,2,0:T(8,128)(2,1)S(1)} all-to-all(bf16[8,256,256]{1,2,0:T(8,128)(2,1)S(1)} %broadcast_in_dim.32), channel_id=1, replica_groups=mesh['rep'=2,'row'=8,'col'=32] {'row'}, dimensions={0} | all-to-all | bytes 2097152 | tf_op jit(solution)/shard_map/all_to_all | solution.py:52
  152.3 0.3 convert_reduce_fusion.2
  152.6 0.3 multiply_reduce_fusion
  152.9 0.4 fusion.17
  153.3 6.1 %fusion.12 = bf16[256,2048]{1,0:T(8,128)(2,1)S(1)} fusion(bf16[2048,3072]{1,0:T(8,128)(2,1)} %all-gather.2.cloned.1.call-done, bf16[256,2048]{0,1:T(8,128)(2,1)S(1)} %fusion.17), kind=kOutput, calls=%fused_computation.17 | convolution fusion | flops 2150367232 | bytes 10485760 | tf_op jit(solution)/shard_map/dot_general | solution.py:65
  159.5 16.1 %all_to_all.22 = bf16[8,256,256]{2,1,0:T(8,128)(2,1)S(1)} all-to-all(bf16[8,256,256]{2,1,0:T(8,128)(2,1)S(1)} %bitcast.82), channel_id=1, replica_groups=mesh['rep'=2,'row'=8,'col'=32] {'row'}, dimensions={0} | all-to-all | bytes 2097152 | tf_op jit(solution)/shard_map/all_to_all | solution.py:60
  175.6 0.1 convert_reduce_fusion
  175.7 0.7 fusion.60
  (33 shorter events, 0.3 us)
Async XLA Ops:
  6.5 19.1 %copy-start = (s32[2,1]{0,1:T(1,128)S(1)}, s32[2,1]{0,1:T(1,128)}, u32[]{:S(2)}) copy-start(s32[2,1]{0,1:T(1,128)} %param.20) | copy-start | bytes 28
  6.5 95.7 %all-gather.2.cloned.1.call-start = ((), (), s32[]{:S(2)}) async-start(), calls=%async_computation.4 | async-start | bytes 12976128 | tf_op jit(solution)/shard_map/all_gather | solution.py:81
  9.2 13.1 %copy-start.7 = (s32[2,1,8]{2,1,0:T(1,128)S(1)}, s32[2,1,8]{2,1,0:T(1,128)}, u32[]{:S(2)}) copy-start(s32[2,1,8]{2,1,0:T(1,128)} %param.19) | copy-start | bytes 196
  11.4 17.2 %all-to-all-start = ((bf16[8,256,256]{1,2,0:T(8,128)(2,1)}), bf16[8,256,256]{1,2,0:T(8,128)(2,1)S(1)}, u32[]{:S(2)}, u32[]{:S(2)}) async-start(bf16[8,256,256]{1,2,0:T(8,128)(2,1)} %broadcast_in_dim.23), calls=%async_computation | async-start | bytes 2097152 | tf_op jit(solution)/shard_map/all_to_all | solution.py:52
  17.3 36.6 %collective-permute-start = (bf16[1,2,8,128,256]{4,3,2,1,0:T(8,128)(2,1)}, bf16[1,2,8,128,256]{4,3,2,1,0:T(8,128)(2,1)}, u32[]{:S(2)}, u32[]{:S(2)}) collective-permute-start(bf16[1,2,8,128,256]{4,3,2,1,0:T(8,128)(2,1)} %param.18), channel_id=1, source_target_pairs={{0,256},{256,0},{1,257},{257,1},{2,258},{258,2},{3,259},{259,3},{4... | collective-permute-start | bytes 3145736 | tf_op jit(solution)/shard_map/ppermute | solution.py:11
  25.6 3.6 %copy-start.5 = (f32[2048]{0:T(1024)S(1)}, f32[2048]{0:T(1024)}, u32[]{:S(2)}) copy-start(f32[2048]{0:T(1024)} %param.16) | copy-start | bytes 24580
  30.6 27.4 %copy-start.2 = (bf16[8,128,256]{2,1,0:T(8,128)(2,1)S(1)}, bf16[8,128,256]{2,1,0:T(8,128)(2,1)}, u32[]{:S(2)}) copy-start(bf16[8,128,256]{2,1,0:T(8,128)(2,1)} %gather_fusion.1) | copy-start | bytes 1572868
  60.2 47.3 %copy-start.3 = (pred[256,1280]{1,0:T(8,128)(4,1)S(1)}, pred[256,1280]{1,0:T(8,128)(4,1)}, u32[]{:S(2)}) copy-start(pred[256,1280]{1,0:T(8,128)(4,1)} %pad_add_fusion) | copy-start | bytes 983044
  108.4 1.5 copy-start.1
  113.2 1.2 slice-start
  114.9 19.9 %copy-start.4 = (bf16[1,1,256,256]{3,2,1,0:T(8,128)(2,1)S(1)}, bf16[1,1,256,256]{3,2,1,0:T(8,128)(2,1)}, u32[]{:S(2)}) copy-start(bf16[1,1,256,256]{3,2,1,0:T(8,128)(2,1)} %param.11) | copy-start | bytes 393220
  135.1 17.9 %copy-start.6 = (f32[2048]{0:T(1024)S(1)}, f32[2048]{0:T(1024)}, u32[]{:S(2)}) copy-start(f32[2048]{0:T(1024)} %param.17) | copy-start | bytes 24580
Sparse Core Ops, SparseCore 0:
  9.5 92.6 all-gather.1

commit v2 on v1

v2 whole, which is shorter than its diff:
```python
import jax
import jax.numpy as jnp
from jax import lax
from jax.experimental import pallas as pl
from jax.experimental.pallas import tpu as pltpu
from jax.sharding import PartitionSpec as P

D = 2048
H = 16


def swapped(value, axis, apart):
    return lax.ppermute(value, axis, [(i, i ^ 1 << apart) for i in range(lax.axis_size(axis))])


def normalize(values, gain):
    mean = jnp.mean(values, axis=-1, keepdims=True)
    centred = values - mean
    spread = jnp.mean(centred * centred, axis=-1, keepdims=True)
    return centred * lax.rsqrt(spread + 1e-05) * gain


def attend_kernel(scalars, slopes, normed, weights, out_weights, keys, values, mixed, total, attn):
    step = pl.program_id(0)
    product = jnp.dot(normed[...], weights[...], preferred_element_type=jnp.float32)

    @pl.when(step == 0)
    def _():
        total[...] = product

    @pl.when(step > 0)
    def _():
        total[...] += product

    @pl.when(step == pl.num_programs(0) - 1)
    def _():
        length = scalars[0]
        seq = normed.shape[0]
        cached = keys.shape[0]
        share = keys.shape[1]
        head_width = D // H
        scale = jnp.float32(head_width) ** -0.5
        cache_pos = lax.broadcasted_iota(jnp.int32, (1, cached), 1)
        cache_ok = cache_pos < length
        cache_off = (cache_pos - length).astype(jnp.float32)
        new_pos = lax.broadcasted_iota(jnp.int32, (seq, seq), 1)
        new_ok = new_pos <= lax.broadcasted_iota(jnp.int32, (seq, seq), 0)
        new_off = lax.broadcasted_iota(jnp.int32, (1, seq), 1).astype(jnp.float32)
        for head in range(share // head_width):
            lanes = slice(head * head_width, (head + 1) * head_width)

            def part(index):
                start = index * share + head * head_width
                return total[:, start : start + head_width].astype(jnp.bfloat16)

            query, new_key, new_value = part(0), part(1), part(2)
            slope = slopes[head]
            cache_score = times_transposed(query, keys[:, lanes]) * scale
            cache_score = jnp.where(cache_ok, cache_score + slope * cache_off, -1e30)
            new_score = times_transposed(query, new_key) * scale
            new_score = jnp.where(new_ok, new_score + slope * new_off, -1e30)
            top = jnp.maximum(
                jnp.max(cache_score, axis=1, keepdims=True),
                jnp.max(new_score, axis=1, keepdims=True),
            )
            cache_weight = jnp.exp(cache_score - top)
            new_weight = jnp.exp(new_score - top)
            whole = jnp.sum(cache_weight, axis=1, keepdims=True) + jnp.sum(
                new_weight, axis=1, keepdims=True
            )
            summed = jnp.dot(
                cache_weight.astype(jnp.bfloat16), values[:, lanes], preferred_element_type=jnp.float32
            ) + jnp.dot(new_weight.astype(jnp.bfloat16), new_value, preferred_element_type=jnp.float32)
            attn[:, lanes] = (summed / whole).astype(jnp.bfloat16)
        for row in range(mixed.shape[0]):
            rows = slice(row * share, (row + 1) * share)
            mixed[row] = times_transposed(attn[...], out_weights[rows, :]).astype(jnp.bfloat16)


def attend(normed, weights, keys, values, length, slopes, rows):
    seq, width = normed.shape
    share = keys.shape[1]
    steps = 4
    deep = width // steps
    return pl.pallas_call(
        attend_kernel,
        out_shape=jax.ShapeDtypeStruct((rows, seq, share), jnp.bfloat16),
        grid_spec=pltpu.PrefetchScalarGridSpec(
            num_scalar_prefetch=2,
            grid=(steps,),
            in_specs=[
                pl.BlockSpec((seq, deep), lambda k, *_: (0, k)),
                pl.BlockSpec((deep, 3 * share), lambda k, *_: (k, 0)),
                pl.BlockSpec((width, share), lambda k, *_: (0, 3)),
                pl.BlockSpec(keys.shape, lambda k, *_: (0, 0)),
                pl.BlockSpec(values.shape, lambda k, *_: (0, 0)),
            ],
            out_specs=pl.BlockSpec((rows, seq, share), lambda k, *_: (0, 0, 0)),
            scratch_shapes=[
                pltpu.VMEM((seq, 3 * share), jnp.float32),
                pltpu.VMEM((seq, share), jnp.bfloat16),
            ],
        ),
        compiler_params=pltpu.CompilerParams(vmem_limit_bytes=48 << 20),
    )(length.reshape(1), slopes, normed, weights, weights, keys, values)


def feed_kernel(state, gain, up_weights, down_weights, down, normed, total):
    step = pl.program_id(0)
    rows, seq, share = state.shape
    width = rows * share

    @pl.when(step == 0)
    def _():
        pieces = [state[row].astype(jnp.float32) for row in range(rows)]
        mean = sum(jnp.sum(piece, axis=1, keepdims=True) for piece in pieces) / width
        centred = [piece - mean for piece in pieces]
        spread = sum(jnp.sum(piece * piece, axis=1, keepdims=True) for piece in centred) / width
        factor = lax.rsqrt(spread + 1e-05)
        for row in range(rows):
            lanes = slice(row * share, (row + 1) * share)
            normed[:, lanes] = (centred[row] * factor * gain[:, lanes]).astype(jnp.bfloat16)

    hidden = jax.nn.gelu(
        jnp.dot(normed[...], up_weights[...], preferred_element_type=jnp.float32), approximate=True
    ).astype(jnp.bfloat16)
    product = times_transposed(hidden, down_weights[...])

    @pl.when(step == 0)
    def _():
        total[...] = product

    @pl.when(step > 0)
    def _():
        total[...] += product

    @pl.when(step == pl.num_programs(0) - 1)
    def _():
        for row in range(rows):
            down[row] = total[:, row * share : (row + 1) * share].astype(jnp.bfloat16)


def feed(state, gain, weights, hidden_share):
    rows, seq, share = state.shape
    width = rows * share
    steps = 4
    each = hidden_share // steps
    up_from = 4 * share // each
    return pl.pallas_call(
        feed_kernel,
        out_shape=jax.ShapeDtypeStruct(state.shape, jnp.bfloat16),
        grid=(steps,),
        in_specs=[
            pl.BlockSpec(state.shape, lambda k: (0, 0, 0)),
            pl.BlockSpec((1, width), lambda k: (0, 0)),
            pl.BlockSpec((width, each), lambda k: (0, up_from + k)),
            pl.BlockSpec((width, each), lambda k: (0, up_from + steps + k)),
        ],
        out_specs=pl.BlockSpec(state.shape, lambda k: (0, 0, 0)),
        scratch_shapes=[
            pltpu.VMEM((seq, width), jnp.bfloat16),
            pltpu.VMEM((seq, width), jnp.float32),
        ],
        compiler_params=pltpu.CompilerParams(vmem_limit_bytes=48 << 20),
    )(state, gain.reshape(1, width), weights, weights)


def row_gather(value):
    copies = jnp.broadcast_to(value[None], (lax.axis_size("row"),) + value.shape)
    return lax.all_to_all(copies, "row", 0, 0, tiled=True)


def row_scatter_sum(parts):
    parts = lax.all_to_all(parts, "row", 0, 0, tiled=True)
    return jnp.sum(parts.astype(jnp.float32), axis=0)


def times_transposed(left, right):
    return lax.dot_general(left, right, (((1,), (1,)), ((), ())), preferred_element_type=jnp.float32)


def local(
    tokens, w_qkv, w_out, w_up, w_down, ln1_gain, ln2_gain, kv_pool, page_table, lengths, moved
):
    rep_index = lax.axis_index("rep")
    row_index = lax.axis_index("row")
    seq = tokens.shape[2]
    share = tokens.shape[3]
    hidden_share = w_up.shape[1]
    head_width = D // H
    heads = share // head_width
    shard = jnp.concatenate(
        [w_qkv.reshape(w_qkv.shape[0], -1), w_out.T, w_up, w_down.T], axis=1
    )
    weights = lax.all_gather(shard, "col", axis=0, tiled=True)
    other = swapped(kv_pool, "rep", 0)
    inputs = tokens.reshape(seq, share)
    rows = jnp.swapaxes(row_gather(inputs), 0, 1).reshape(seq, D)
    normed = normalize(rows.astype(jnp.float32), ln1_gain).astype(jnp.bfloat16)
    head_ids = (row_index * heads + jnp.arange(heads, dtype=jnp.int32) + 1).astype(jnp.float32)
    slopes = 2.0 ** (-8.0 * head_ids / H)

    def pages_of(store, table):
        return store[table].reshape(-1, store.shape[2])

    flag = moved[0] == 1
    home = jnp.where(flag, 1 - rep_index, rep_index)
    table = page_table[home, 0]
    length = lengths[home, 0]
    cache_keys = jnp.where(flag, pages_of(other[0, 0], table), pages_of(kv_pool[0, 0], table))
    cache_values = jnp.where(flag, pages_of(other[0, 1], table), pages_of(kv_pool[0, 1], table))
    partial_mix = attend(
        normed, weights, cache_keys, cache_values, length, slopes, lax.axis_size("row")
    )
    mixed = row_scatter_sum(partial_mix)
    state_local = (inputs.astype(jnp.float32) + mixed).astype(jnp.bfloat16)
    down = row_scatter_sum(feed(row_gather(state_local), ln2_gain, weights, hidden_share))
    finished = (state_local.astype(jnp.float32) + down).astype(jnp.bfloat16)
    return finished.reshape(tokens.shape)


def solution(mesh):
    return jax.shard_map(
        local,
        mesh=mesh,
        in_specs=(
            P("rep", "col", None, "row"),
            P("col", None, "row"),
            P("row", "col"),
            P("col", "row"),
            P("row", "col"),
            P(),
            P(),
            P("rep", None, "col", None, "row"),
            P(None, "col", None),
            P(None, "col"),
            P("col"),
        ),
        out_specs=P("rep", "col", None, "row"),
        check_vma=False,
    )
```

time: 185 us -> 181 us (0.978)
  Pallas kernels: 0 us -> 15.7 us
  matrix products: 14.7 us -> 0 us
  other arithmetic: 10.4 us -> 4.2 us
  waiting for transfers between devices: 65.3 us -> 71.2 us
  local copies, waits for them, and re-layouts: 15.1 us -> 10.4 us
    pallas_call x0 -> x2, Pallas kernels: none -> 15.7 us  [the longest x1 8.59 us: feed(): pl.pallas_call(feed_kernel, out_shape=jax.ShapeDtypeStruct(state.shape, j...]
    dot_general x5 -> x0, matrix products: 14.7 us -> none  [the longest x2 6.56 us: times_transposed(): lax.dot_general(left, right, (((1,), (1,)), ((), ())), preferred_element_...]
    all_to_all x1, waiting for transfers between devices: 0.01 us -> 2.96 us  [row_gather(): return lax.all_to_all(copies, 'row', 0, 0, tiled=True)]
    all_gather x1, waiting for transfers between devices: 42 us -> 44.2 us  [local(): weights = lax.all_gather(shard, 'col', axis=0, tiled=True)]
  transfers between devices with their start and end apart: 3 -> 3, of which waited for: 2 -> 3; matrix products, arithmetic and copies ran while one was open for 9% -> 6% of each run, Pallas kernels for 0% -> 0%
where the time goes in v2:
time: 181 us; the launch traced here: 179 us
  waiting for transfers between devices  71.2 us (39%)
  blocking collectives  52.9 us (29%)
  Pallas kernels  15.7 us (9%)
  between operations  14.2 us (8%)
  local copies, waits for them, and re-layouts  10.4 us (6%)
  starting transfers between devices  10.3 us (6%)
  other arithmetic  4.2 us (2%)
    all_gather x1, waiting for transfers between devices, local(): weights = lax.all_gather(shard, 'col', axis=0, tiled=True)  44.2 us
    all_to_all x2, blocking collectives, row_scatter_sum(): parts = lax.all_to_all(parts, 'row', 0, 0, tiled=True)  35.7 us
    ppermute x1, waiting for transfers between devices, swapped(): lax.ppermute(value, axis, [(i, i ^ 1 << apart) for i in range(lax.axis_si...  24 us
    all_to_all x1, blocking collectives, row_gather(): return lax.all_to_all(copies, 'row', 0, 0, tiled=True)  17.2 us
    pallas_call x1, Pallas kernels, feed(): pl.pallas_call(feed_kernel, out_shape=jax.ShapeDtypeStruct(state.shape, j...  8.59 us
    pallas_call x1, Pallas kernels, attend(): pl.pallas_call(attend_kernel, out_shape=jax.ShapeDtypeStruct((rows, seq,...  7.1 us
    all_to_all x1, starting transfers between devices, row_gather(): return lax.all_to_all(copies, 'row', 0, 0, tiled=True)  5.95 us
    ppermute x1, starting transfers between devices, swapped(): lax.ppermute(value, axis, [(i, i ^ 1 << apart) for i in range(lax.axis_si...  4.35 us
  transfers between devices with their start and end apart: 3, of which 3 were waited for; matrix products, arithmetic and copies ran while one was open for 6% of the time, Pallas kernels for 0%

profile of v2, /device:TPU:1, one launch (start us, length us, event | category | flops | bytes accessed | tf_op | source)
XLA Modules:
  0.0 179.0 jit_solution(1310484306304704920)
XLA Ops:
  6.5 0.0 copy-start
  6.5 0.0 all-gather.2.cloned.1.call-start
  6.5 0.9 copy.17
  7.5 0.0 copy-start.4
  7.5 1.8 pad_maximum_fusion
  9.2 0.0 all-gather.2.cloned.1.call-update
  9.2 2.0 %broadcast_in_dim.7 = bf16[8,256,256]{2,1,0:T(8,128)(2,1)} broadcast(bf16[256,256]{1,0:T(8,128)(2,1)} %bitcast.41), dimensions={1,2} | broadcast | bytes 1179648 | tf_op jit(solution)/shard_map/broadcast_in_dim | solution.py:169
  11.3 5.9 %all-to-all-start = ((bf16[8,256,256]{2,1,0:T(8,128)(2,1)}), bf16[8,256,256]{2,1,0:T(8,128)(2,1)S(1)}, u32[]{:S(2)}, u32[]{:S(2)}) async-start(bf16[8,256,256]{2,1,0:T(8,128)(2,1)} %broadcast_in_dim.7), calls=%async_computation | async-start | bytes 2097152 | tf_op jit(solution)/shard_map/all_to_all | solution.py:170
  17.2 4.3 %collective-permute-start = (bf16[1,2,8,128,256]{4,3,2,1,0:T(8,128)(2,1)}, bf16[1,2,8,128,256]{4,3,2,1,0:T(8,128)(2,1)}, u32[]{:S(2)}, u32[]{:S(2)}) collective-permute-start(bf16[1,2,8,128,256]{4,3,2,1,0:T(8,128)(2,1)} %param.18), channel_id=1, source_target_pairs={{0,256},{256,0},{1,257},{257,1},{2,258},{258,2},{3,259},{259,3},{4... | collective-permute-start | bytes 3145736 | tf_op jit(solution)/shard_map/ppermute | solution.py:13
  22.2 0.0 copy-done.4
  22.3 1.3 slice_bitcast_fusion.2
  23.5 0.6 gather_fusion.1
  24.1 0.6 gather_fusion.3
  24.7 0.0 copy-done
  24.7 0.6 constant_dynamic-slice_fusion
  25.4 3.0 %all-to-all-done = bf16[8,256,256]{2,1,0:T(8,128)(2,1)S(1)} async-done(((bf16[8,256,256]{2,1,0:T(8,128)(2,1)}), bf16[8,256,256]{2,1,0:T(8,128)(2,1)S(1)}, u32[]{:S(2)}, u32[]{:S(2)}) %all-to-all-start) | async-done | bytes 1048608 | tf_op jit(solution)/shard_map/all_to_all | solution.py:170
  28.3 0.2 convert_reduce_fusion
  28.5 0.2 convert_bitcast_fusion
  28.7 0.0 copy-start.3
  28.7 0.3 copy.16
  29.0 0.4 fusion.1
  29.5 0.0 copy-done.3
  29.5 0.4 multiply_convert_fusion.normed
  29.8 24.0 %collective-permute-done = bf16[1,2,8,128,256]{4,3,2,1,0:T(8,128)(2,1)} collective-permute-done((bf16[1,2,8,128,256]{4,3,2,1,0:T(8,128)(2,1)}, bf16[1,2,8,128,256]{4,3,2,1,0:T(8,128)(2,1)}, u32[]{:S(2)}, u32[]{:S(2)}) %collective-permute-start) | collective-permute-done | bytes 1048608 | tf_op jit(solution)/shard_map/ppermute | solution.py:13
  53.8 1.3 slice_bitcast_fusion
  55.1 1.4 gather_fusion
  56.5 1.4 gather_fusion.2
  57.9 0.2 broadcast_select_fusion
  58.1 44.2 %all-gather.2.cloned.1.call-done.weights.out_weights.up_weights.down_weights = bf16[2048,3072]{1,0:T(8,128)(2,1)} async-done(((bf16[64,3072]{1,0:T(8,128)(2,1)}), bf16[2048,3072]{1,0:T(8,128)(2,1)}) %all-gather.2.cloned.1.call-update) | async-done | bytes 12582928 | tf_op jit(solution)/shard_map/all_gather | solution.py:195
  102.3 7.1 %shard_map.109 = bf16[8,256,256]{2,1,0:T(8,128)(2,1)S(1)} custom-call(s32[1]{0:T(128)} %bitcast.1.scalars, f32[2]{0:T(128)S(1)} %multiply_power_fusion.slopes, bf16[256,2048]{1,0:T(8,128)(2,1)S(1)} %multiply_convert_fusion.normed, bf16[2048,3072]{1,0:T(8,128)(2,1)} %all-gather.2.cloned.1.call-done.weights.out_weights.up_weights.down_weights, ...), custom_call_target="tpu_custom_call" | custom-call | tf_op jit(solution)/shard_map/pallas_call | solution.py:85
  109.4 0.0 copy-start.2
  109.4 19.7 %all_to_all.20 = bf16[8,256,256]{2,1,0:T(8,128)(2,1)S(1)} all-to-all(bf16[8,256,256]{2,1,0:T(8,128)(2,1)S(1)} %shard_map.109), channel_id=1, replica_groups=mesh['rep'=2,'row'=8,'col'=32] {'row'}, dimensions={0} | all-to-all | bytes 2097152 | tf_op jit(solution)/shard_map/all_to_all | solution.py:174
  129.1 0.1 convert_reduce_fusion.2
  129.2 0.0 copy-done.2
  129.3 0.0 copy-start.1
  129.3 0.1 broadcast_in_dim.8
  129.4 17.2 %all_to_all.21.state = bf16[8,256,256]{2,1,0:T(8,128)(2,1)S(1)} all-to-all(bf16[8,256,256]{2,1,0:T(8,128)(2,1)S(1)} %broadcast_in_dim.8), channel_id=1, replica_groups=mesh['rep'=2,'row'=8,'col'=32] {'row'}, dimensions={0} | all-to-all | bytes 2097152 | tf_op jit(solution)/shard_map/all_to_all | solution.py:170
  146.6 0.0 copy-done.1
  146.6 8.6 %shard_map.110 = bf16[8,256,256]{2,1,0:T(8,128)(2,1)S(1)} custom-call(bf16[8,256,256]{2,1,0:T(8,128)(2,1)S(1)} %all_to_all.21.state, f32[1,2048]{1,0:T(1,128)S(1)} %bitcast.39, bf16[2048,3072]{1,0:T(8,128)(2,1)} %all-gather.2.cloned.1.call-done.weights.out_weights.up_weights.down_weights, ...), custom_call_target="tpu_custom_call" | custom-call | tf_op jit(solution)/shard_map/pallas_call | solution.py:149
  155.2 16.1 %all_to_all.22 = bf16[8,256,256]{2,1,0:T(8,128)(2,1)S(1)} all-to-all(bf16[8,256,256]{2,1,0:T(8,128)(2,1)S(1)} %shard_map.110), channel_id=1, replica_groups=mesh['rep'=2,'row'=8,'col'=32] {'row'}, dimensions={0} | all-to-all | bytes 2097152 | tf_op jit(solution)/shard_map/all_to_all | solution.py:174
  171.3 0.1 convert_reduce_fusion.1
  171.4 0.7 fusion.2
  (6 shorter events, 0.1 us)
Async XLA Ops:
  6.5 18.2 %copy-start = (s32[2,1]{0,1:T(1,128)S(1)}, s32[2,1]{0,1:T(1,128)}, u32[]{:S(2)}) copy-start(s32[2,1]{0,1:T(1,128)} %param.20) | copy-start | bytes 28
  6.5 95.8 %all-gather.2.cloned.1.call-start = ((), (), s32[]{:S(2)}) async-start(), calls=%async_computation.4 | async-start | bytes 12976128 | tf_op jit(solution)/shard_map/all_gather | solution.py:195
  7.5 14.8 %copy-start.4 = (s32[2,1,8]{2,1,0:T(1,128)S(1)}, s32[2,1,8]{2,1,0:T(1,128)}, u32[]{:S(2)}) copy-start(s32[2,1,8]{2,1,0:T(1,128)} %param.19) | copy-start | bytes 196
  11.3 17.0 %all-to-all-start = ((bf16[8,256,256]{2,1,0:T(8,128)(2,1)}), bf16[8,256,256]{2,1,0:T(8,128)(2,1)S(1)}, u32[]{:S(2)}, u32[]{:S(2)}) async-start(bf16[8,256,256]{2,1,0:T(8,128)(2,1)} %broadcast_in_dim.7), calls=%async_computation | async-start | bytes 2097152 | tf_op jit(solution)/shard_map/all_to_all | solution.py:170
  17.2 36.6 %collective-permute-start = (bf16[1,2,8,128,256]{4,3,2,1,0:T(8,128)(2,1)}, bf16[1,2,8,128,256]{4,3,2,1,0:T(8,128)(2,1)}, u32[]{:S(2)}, u32[]{:S(2)}) collective-permute-start(bf16[1,2,8,128,256]{4,3,2,1,0:T(8,128)(2,1)} %param.18), channel_id=1, source_target_pairs={{0,256},{256,0},{1,257},{257,1},{2,258},{258,2},{3,259},{259,3},{4... | collective-permute-start | bytes 3145736 | tf_op jit(solution)/shard_map/ppermute | solution.py:13
  28.7 0.7 copy-start.3
  109.4 19.8 %copy-start.2 = (bf16[1,1,256,256]{3,2,1,0:T(8,128)(2,1)S(1)}, bf16[1,1,256,256]{3,2,1,0:T(8,128)(2,1)}, u32[]{:S(2)}) copy-start(bf16[1,1,256,256]{3,2,1,0:T(8,128)(2,1)} %param.11) | copy-start | bytes 393220
  129.3 17.3 %copy-start.1 = (f32[2048]{0:T(1024)S(1)}, f32[2048]{0:T(1024)}, u32[]{:S(2)}) copy-start(f32[2048]{0:T(1024)} %param.17) | copy-start | bytes 24580
Sparse Core Ops, SparseCore 0:
  9.5 92.7 all-gather.1

commit v3 on v2

v3 whole, which is shorter than its diff:
```python
import jax
import jax.numpy as jnp
from jax import lax
from jax.experimental import pallas as pl
from jax.experimental.pallas import tpu as pltpu
from jax.sharding import Mesh
from jax.sharding import PartitionSpec as P

D = 2048
H = 16


def swapped(value, axis, apart):
    return lax.ppermute(value, axis, [(i, i ^ 1 << apart) for i in range(lax.axis_size(axis))])


def normalize(values, gain):
    mean = jnp.mean(values, axis=-1, keepdims=True)
    centred = values - mean
    spread = jnp.mean(centred * centred, axis=-1, keepdims=True)
    return centred * lax.rsqrt(spread + 1e-05) * gain


def attend_kernel(scalars, slopes, normed, weights, keys, values, copies, total, attn):
    step = pl.program_id(0)
    product = jnp.dot(normed[...], weights[...], preferred_element_type=jnp.float32)

    @pl.when(step == 0)
    def _():
        total[...] = product

    @pl.when(step > 0)
    def _():
        total[...] += product

    @pl.when(step == pl.num_programs(0) - 1)
    def _():
        length = scalars[0]
        seq = normed.shape[0]
        cached = keys.shape[0]
        share = keys.shape[1]
        head_width = D // H
        scale = jnp.float32(head_width) ** -0.5
        cache_pos = lax.broadcasted_iota(jnp.int32, (1, cached), 1)
        cache_ok = cache_pos < length
        cache_off = (cache_pos - length).astype(jnp.float32)
        new_pos = lax.broadcasted_iota(jnp.int32, (seq, seq), 1)
        new_ok = new_pos <= lax.broadcasted_iota(jnp.int32, (seq, seq), 0)
        new_off = lax.broadcasted_iota(jnp.int32, (1, seq), 1).astype(jnp.float32)
        for head in range(share // head_width):
            lanes = slice(head * head_width, (head + 1) * head_width)

            def part(index):
                start = index * share + head * head_width
                return total[:, start : start + head_width].astype(jnp.bfloat16)

            query, new_key, new_value = part(0), part(1), part(2)
            slope = slopes[head]
            cache_score = times_transposed(query, keys[:, lanes]) * scale
            cache_score = jnp.where(cache_ok, cache_score + slope * cache_off, -1e30)
            new_score = times_transposed(query, new_key) * scale
            new_score = jnp.where(new_ok, new_score + slope * new_off, -1e30)
            top = jnp.maximum(
                jnp.max(cache_score, axis=1, keepdims=True),
                jnp.max(new_score, axis=1, keepdims=True),
            )
            cache_weight = jnp.exp(cache_score - top)
            new_weight = jnp.exp(new_score - top)
            whole = jnp.sum(cache_weight, axis=1, keepdims=True) + jnp.sum(
                new_weight, axis=1, keepdims=True
            )
            summed = jnp.dot(
                cache_weight.astype(jnp.bfloat16), values[:, lanes], preferred_element_type=jnp.float32
            ) + jnp.dot(new_weight.astype(jnp.bfloat16), new_value, preferred_element_type=jnp.float32)
            attn[:, lanes] = (summed / whole).astype(jnp.bfloat16)
        for row in range(copies.shape[0]):
            copies[row] = attn[...]


def attend(normed, weights, keys, values, length, slopes, rows):
    seq, width = normed.shape
    share = keys.shape[1]
    steps = 4
    deep = width // steps
    return pl.pallas_call(
        attend_kernel,
        out_shape=jax.ShapeDtypeStruct((rows, seq, share), jnp.bfloat16),
        grid_spec=pltpu.PrefetchScalarGridSpec(
            num_scalar_prefetch=2,
            grid=(steps,),
            in_specs=[
                pl.BlockSpec((seq, deep), lambda k, *_: (0, k)),
                pl.BlockSpec((deep, 3 * share), lambda k, *_: (k, 0)),
                pl.BlockSpec(keys.shape, lambda k, *_: (0, 0)),
                pl.BlockSpec(values.shape, lambda k, *_: (0, 0)),
            ],
            out_specs=pl.BlockSpec((rows, seq, share), lambda k, *_: (0, 0, 0)),
            scratch_shapes=[
                pltpu.VMEM((seq, 3 * share), jnp.float32),
                pltpu.VMEM((seq, share), jnp.bfloat16),
            ],
        ),
        compiler_params=pltpu.CompilerParams(vmem_limit_bytes=48 << 20),
    )(length.reshape(1), slopes, normed, weights, keys, values)


def feed_kernel(place, attns, tokens, gain, near, far, gathered, down, state_local,
                out_weights, feed_weights, wide, state, hidden, sems):
    rows, seq, share = attns.shape
    width = rows * share
    hidden_share = feed_weights.shape[2]
    chips = near.shape[1]
    first = 3 * share
    copies = []

    def copy(source, target):
        copies.append(pltpu.make_async_copy(source, target, sems.at[len(copies)]))
        copies[-1].start()

    for row in range(rows):
        lanes = pl.ds(row * share, share)
        copy(near.at[row], out_weights.at[:, place[0], :, lanes])
        copy(far.at[row], out_weights.at[:, 1 - place[0], :, lanes])
    for part in range(2):
        copy(gathered.at[:, pl.ds(first + part * hidden_share, hidden_share)], feed_weights.at[part])
    for row in range(rows):
        wide[:, row * share : (row + 1) * share] = attns[row]
    for item in copies[: 2 * rows]:
        item.wait()
    each = chips // rows
    for row in range(rows):
        block = out_weights[row * each : (row + 1) * each].reshape(share, width)
        mixed = times_transposed(wide[...], block)
        state[row] = (tokens[row].astype(jnp.float32) + mixed).astype(jnp.bfloat16)
    state_local[...] = state[place[1]]
    pieces = [state[row].astype(jnp.float32) for row in range(rows)]
    mean = sum(jnp.sum(piece, axis=1, keepdims=True) for piece in pieces) / width
    centred = [piece - mean for piece in pieces]
    spread = sum(jnp.sum(piece * piece, axis=1, keepdims=True) for piece in centred) / width
    factor = lax.rsqrt(spread + 1e-05)
    for row in range(rows):
        lanes = slice(row * share, (row + 1) * share)
        wide[:, lanes] = (centred[row] * factor * gain[:, lanes]).astype(jnp.bfloat16)
    copies[2 * rows].wait()
    for part in range(4):
        lanes = slice(part * hidden_share // 4, (part + 1) * hidden_share // 4)
        up = jnp.dot(wide[...], feed_weights[0, :, lanes], preferred_element_type=jnp.float32)
        hidden[:, lanes] = jax.nn.gelu(up, approximate=True).astype(jnp.bfloat16)
    copies[2 * rows + 1].wait()
    for row in range(rows):
        lanes = slice(row * share, (row + 1) * share)
        down[row] = times_transposed(hidden[...], feed_weights[1, lanes, :]).astype(jnp.bfloat16)


def feed(place, attns, tokens, gain, near, far, gathered, hidden_share):
    rows, seq, share = attns.shape
    width = rows * share
    chips = near.shape[1]
    return pl.pallas_call(
        feed_kernel,
        out_shape=(
            jax.ShapeDtypeStruct(attns.shape, jnp.bfloat16),
            jax.ShapeDtypeStruct((seq, share), jnp.bfloat16),
        ),
        grid_spec=pltpu.PrefetchScalarGridSpec(
            num_scalar_prefetch=1,
            grid=(1,),
            in_specs=[
                pl.BlockSpec(attns.shape, lambda *_: (0, 0, 0)),
                pl.BlockSpec(tokens.shape, lambda *_: (0, 0, 0)),
                pl.BlockSpec((1, width), lambda *_: (0, 0)),
                pl.BlockSpec(memory_space=pl.ANY),
                pl.BlockSpec(memory_space=pl.ANY),
                pl.BlockSpec(memory_space=pl.ANY),
            ],
            out_specs=(
                pl.BlockSpec(attns.shape, lambda *_: (0, 0, 0)),
                pl.BlockSpec((seq, share), lambda *_: (0, 0)),
            ),
            scratch_shapes=[
                pltpu.VMEM((chips, 2, width // chips // 2, width), jnp.bfloat16),
                pltpu.VMEM((2, width, hidden_share), jnp.bfloat16),
                pltpu.VMEM((seq, width), jnp.bfloat16),
                pltpu.VMEM(attns.shape, jnp.bfloat16),
                pltpu.VMEM((seq, hidden_share), jnp.bfloat16),
                pltpu.SemaphoreType.DMA((2 * rows + 2,)),
            ],
        ),
        compiler_params=pltpu.CompilerParams(vmem_limit_bytes=48 << 20),
    )(place, attns, tokens, gain.reshape(1, width), near, far, gathered)


def row_exchange(parts):
    return lax.all_to_all(parts, "row", 0, 0, tiled=True)


def row_gather(value):
    return row_exchange(jnp.broadcast_to(value[None], (lax.axis_size("row"),) + value.shape))


def row_scatter_sum(parts):
    parts = row_exchange(parts)
    return jnp.sum(parts.astype(jnp.float32), axis=0)


def times_transposed(left, right):
    return lax.dot_general(left, right, (((1,), (1,)), ((), ())), preferred_element_type=jnp.float32)


def local(
    tokens, w_qkv, w_out, w_up, w_down, ln1_gain, ln2_gain, kv_pool, page_table, lengths, moved
):
    rep_index = lax.axis_index("rep")
    row_index = lax.axis_index("row")
    seq = tokens.shape[2]
    share = tokens.shape[3]
    hidden_share = w_up.shape[1]
    head_width = D // H
    heads = share // head_width
    inputs = tokens.reshape(seq, share)
    spread_tokens = row_gather(inputs)
    shard = jnp.concatenate([w_qkv.reshape(w_qkv.shape[0], -1), w_up, w_down.T], axis=1)
    weights = lax.all_gather(shard, ("z", "core"), axis=0, tiled=True)
    other = swapped(kv_pool, "rep", 0)
    out_block = lax.all_gather(w_out.T, "z", axis=0, tiled=False)
    out_block, spread_tokens, other = lax.optimization_barrier((out_block, spread_tokens, other))
    near = row_gather(out_block)
    rows = jnp.swapaxes(spread_tokens, 0, 1).reshape(seq, D)
    normed = normalize(rows.astype(jnp.float32), ln1_gain).astype(jnp.bfloat16)
    head_ids = (row_index * heads + jnp.arange(heads, dtype=jnp.int32) + 1).astype(jnp.float32)
    slopes = 2.0 ** (-8.0 * head_ids / H)

    def pages_of(store, table):
        return store[table].reshape(-1, store.shape[2])

    flag = moved[0] == 1
    home = jnp.where(flag, 1 - rep_index, rep_index)
    table = page_table[home, 0]
    length = lengths[home, 0]
    cache_keys = jnp.where(flag, pages_of(other[0, 0], table), pages_of(kv_pool[0, 0], table))
    cache_values = jnp.where(flag, pages_of(other[0, 1], table), pages_of(kv_pool[0, 1], table))
    attn_copies = attend(
        normed, weights, cache_keys, cache_values, length, slopes, lax.axis_size("row")
    )
    attns = row_exchange(attn_copies)
    near, _ = lax.optimization_barrier((near, attn_copies))
    far = swapped(near, "core", 0)
    place = jnp.stack([lax.axis_index("core"), row_index]).astype(jnp.int32)
    partial_down, state_local = feed(
        place, attns, spread_tokens, ln2_gain, near, far, weights, hidden_share
    )
    down = row_scatter_sum(partial_down)
    finished = (state_local.astype(jnp.float32) + down).astype(jnp.bfloat16)
    return finished.reshape(tokens.shape)


def solution(mesh):
    reps, rows, cols = mesh.devices.shape
    mesh = Mesh(mesh.devices.reshape(reps, rows, cols // 2, 2), ("rep", "row", "z", "core"))
    col = ("z", "core")
    return jax.shard_map(
        local,
        mesh=mesh,
        in_specs=(
            P("rep", col, None, "row"),
            P(col, None, "row"),
            P("row", col),
            P(col, "row"),
            P("row", col),
            P(),
            P(),
            P("rep", None, col, None, "row"),
            P(None, col, None),
            P(None, col),
            P(col),
        ),
        out_specs=P("rep", col, None, "row"),
        check_vma=False,
    )
```

time: 181 us -> 176 us (0.972)
  waiting for transfers between devices: 71.2 us -> 36.8 us
  starting transfers between devices: 10.3 us -> 27.8 us
  local copies, waits for them, and re-layouts: 10.4 us -> 18.2 us
  blocking collectives: 52.9 us -> 55.8 us
    all_gather x0 -> x1, blocking collectives: none -> 38.4 us  [local(): out_block = lax.all_gather(w_out.T, 'z', axis=0, tiled=False)]
    all_to_all x3 -> x1, blocking collectives: 52.9 us -> 17.4 us  [row_exchange(): return lax.all_to_all(parts, 'row', 0, 0, tiled=True)]
    all_gather x1, waiting for transfers between devices: 44.2 us -> 19.2 us  [local(): weights = lax.all_gather(shard, ('z', 'core'), axis=0, tiled=True)]
    ppermute x1 -> x2, waiting for transfers between devices: 24 us -> 0.01 us  [swapped(): lax.ppermute(value, axis, [(i, i ^ 1 << apart) for i in range(lax.axis_si...]
    all_to_all x1 -> x3, waiting for transfers between devices: 2.96 us -> 17.6 us  [row_exchange(): return lax.all_to_all(parts, 'row', 0, 0, tiled=True)]
    ppermute x1 -> x2, starting transfers between devices: 4.35 us -> 14.2 us  [swapped(): lax.ppermute(value, axis, [(i, i ^ 1 << apart) for i in range(lax.axis_si...]
    all_to_all x1 -> x3, starting transfers between devices: 5.95 us -> 13.6 us  [row_exchange(): return lax.all_to_all(parts, 'row', 0, 0, tiled=True)]
    convert_element_type x1 -> x2, local copies, waits for them, and re-layouts: 0.27 us -> 3.8 us  [local(): normed = normalize(rows.astype(jnp.float32), ln1_gain).astype(jnp.bfloat16)]
  transfers between devices with their start and end apart: 3 -> 6, of which waited for: 3 -> 3; matrix products, arithmetic and copies ran while one was open for 6% -> 10% of each run, Pallas kernels for 0% -> 4%
where the time goes in v3:
time: 176 us; the launch traced here: 175 us
  blocking collectives  55.8 us (32%)
  waiting for transfers between devices  36.8 us (21%)
  starting transfers between devices  27.8 us (16%)
  local copies, waits for them, and re-layouts  18.2 us (10%)
  Pallas kernels  17.2 us (10%)
  between operations  14.2 us (8%)
  other arithmetic  5.33 us (3%)
    all_gather x1, blocking collectives, local(): out_block = lax.all_gather(w_out.T, 'z', axis=0, tiled=False)  38.4 us
    all_gather x1, waiting for transfers between devices, local(): weights = lax.all_gather(shard, ('z', 'core'), axis=0, tiled=True)  19.2 us
    all_to_all x3, waiting for transfers between devices, row_exchange(): return lax.all_to_all(parts, 'row', 0, 0, tiled=True)  17.6 us
    all_to_all x1, blocking collectives, row_exchange(): return lax.all_to_all(parts, 'row', 0, 0, tiled=True)  17.4 us
    ppermute x2, starting transfers between devices, swapped(): lax.ppermute(value, axis, [(i, i ^ 1 << apart) for i in range(lax.axis_si...  14.2 us
    all_to_all x3, starting transfers between devices, row_exchange(): return lax.all_to_all(parts, 'row', 0, 0, tiled=True)  13.6 us
    pallas_call x1, Pallas kernels, feed(): pl.pallas_call(feed_kernel, out_shape=(jax.ShapeDtypeStruct(attns.shape,...  9.83 us
    pallas_call x1, Pallas kernels, attend(): pl.pallas_call(attend_kernel, out_shape=jax.ShapeDtypeStruct((rows, seq,...  7.41 us
  transfers between devices with their start and end apart: 6, of which 3 were waited for; matrix products, arithmetic and copies ran while one was open for 10% of the time, Pallas kernels for 4%

profile of v3, /device:TPU:1, one launch (start us, length us, event | category | flops | bytes accessed | tf_op | source)
XLA Modules:
  0.0 175.4 jit_solution(13155943584760023594)
XLA Ops:
  6.5 0.9 copy.16
  7.5 1.7 pad_maximum_fusion
  9.2 0.0 all-gather.3.cloned.1.call-update
  9.2 5.5 %collective-permute-start = (bf16[1,2,8,128,256]{4,3,2,1,0:T(8,128)(2,1)}, bf16[1,2,8,128,256]{4,3,2,1,0:T(8,128)(2,1)S(1)}, u32[]{:S(2)}, u32[]{:S(2)}) collective-permute-start(bf16[1,2,8,128,256]{4,3,2,1,0:T(8,128)(2,1)} %param.18), channel_id=1, source_target_pairs={{0,256},{256,0},{1,257},{257,1},{2,258},{258,2},{3,259},{259,3},{4... | collective-permute-start | bytes 3145736 | tf_op jit(solution)/shard_map/ppermute | solution.py:14
  14.7 2.0 %broadcast_in_dim.7 = bf16[8,256,256]{2,1,0:T(8,128)(2,1)} broadcast(bf16[256,256]{1,0:T(8,128)(2,1)} %bitcast.36), dimensions={1,2} | broadcast | bytes 1179648 | tf_op jit(solution)/shard_map/broadcast_in_dim | solution.py:198
  16.7 4.2 %all-to-all-start = ((bf16[8,256,256]{2,1,0:T(8,128)(2,1)}), bf16[8,256,256]{2,1,0:T(8,128)(2,1)S(1)}, u32[]{:S(2)}, u32[]{:S(2)}) async-start(bf16[8,256,256]{2,1,0:T(8,128)(2,1)} %broadcast_in_dim.7), calls=%async_computation | async-start | bytes 2097152 | tf_op jit(solution)/shard_map/all_to_all | solution.py:194
  20.9 0.0 copy-done.10
  20.9 38.4 %all-gather = bf16[1024,256]{1,0:T(8,128)(2,1)S(1)} all-gather(bf16[64,256]{1,0:T(8,128)(2,1)S(1)} %bitcast.39), channel_id=2, replica_groups=mesh['rep'=2,'row'=8,'z'=16,'core'=2] {'z'}, dimensions={0}, use_global_device_ids=true | all-gather | bytes 557056 | tf_op jit(solution)/shard_map/all_gather | solution.py:225
  59.3 0.0 all-to-all-done.tokens
  59.4 0.0 collective-permute-done
  59.4 1.0 copy-done.8
  60.4 2.5 %broadcast_in_dim.8 = bf16[8,16,64,256]{3,2,1,0:T(8,128)(2,1)} broadcast(bf16[16,64,256]{2,1,0:T(8,128)(2,1)S(1)} %bitcast.34), dimensions={1,2,3} | broadcast | bytes 4718592 | tf_op jit(solution)/shard_map/broadcast_in_dim | solution.py:198
  62.9 5.8 %all-to-all-start.2 = ((bf16[8,16,64,256]{3,2,1,0:T(8,128)(2,1)}), bf16[8,16,64,256]{3,2,1,0:T(8,128)(2,1)}, u32[]{:S(2)}, u32[]{:S(2)}) async-start(bf16[8,16,64,256]{3,2,1,0:T(8,128)(2,1)} %broadcast_in_dim.8), calls=%async_computation.2 | async-start | bytes 8388608 | tf_op jit(solution)/shard_map/all_to_all | solution.py:194
  69.4 0.6 constant_dynamic-slice_fusion
  70.0 0.1 slice_bitcast_fusion
  70.1 0.0 copy-start.9
  70.1 1.4 gather_fusion.3
  71.5 1.4 gather_fusion.1
  72.9 0.0 copy-done.9
  72.9 0.1 slice_bitcast_fusion.1
  73.0 1.4 gather_fusion.2
  74.4 1.4 gather_fusion
  75.8 1.5 convert_bitcast_fusion
  77.3 1.9 %copy.13 = f32[256,8,256]{0,2,1:T(8,128)S(1)} copy(f32[256,8,256]{2,0,1:T(8,128)} %convert_bitcast_fusion) | data formatting | bytes 4194304 | tf_op jit(solution)/shard_map/convert_element_type | solution.py:229
  79.3 1.9 %copy.14 = f32[256,2048]{1,0:T(8,128)} copy(f32[256,2048]{0,1:T(8,128)S(1)} %bitcast.33) | data formatting | bytes 4194304 | tf_op jit(solution)/shard_map/convert_element_type | solution.py:229
  81.2 0.2 convert_reduce_fusion
  81.4 0.0 copy-start.11
  81.4 0.4 fusion.1
  81.8 0.4 copy-done.3
  82.2 0.2 copy-done.4
  82.3 0.2 copy-done.5
  82.5 0.2 copy-done.6
  82.7 0.1 broadcast_select_fusion
  82.8 0.7 copy-done.2
  83.5 0.4 multiply_convert_fusion.normed
  83.9 19.2 %all-gather.3.cloned.1.call-done.weights.gathered = bf16[2048,2816]{1,0:T(8,128)(2,1)} async-done(((bf16[64,2816]{1,0:T(8,128)(2,1)}), bf16[2048,2816]{1,0:T(8,128)(2,1)}) %all-gather.3.cloned.1.call-update) | async-done | bytes 11534352 | tf_op jit(solution)/shard_map/all_gather | solution.py:223
  103.1 7.4 %shard_map.109 = bf16[8,256,256]{2,1,0:T(8,128)(2,1)} custom-call(s32[1]{0:T(128)} %bitcast.3.scalars, f32[2]{0:T(128)S(1)} %multiply_power_fusion.slopes, bf16[256,2048]{1,0:T(8,128)(2,1)S(1)} %multiply_convert_fusion.normed, bf16[2048,2816]{1,0:T(8,128)(2,1)} %all-gather.3.cloned.1.call-done.weights.gathered, bf16[1024,256]{1,0:T(8,128)(2,1)S(1)} %bitcast.31, ...), custom_call_target="tpu_custom_call" | custom-call | tf_op jit(solution)/shard_map/pallas_call | solution.py:85
  110.5 1.8 %all-to-all-done.2.near = bf16[8,16,64,256]{3,2,1,0:T(8,128)(2,1)} async-done(((bf16[8,16,64,256]{3,2,1,0:T(8,128)(2,1)}), bf16[8,16,64,256]{3,2,1,0:T(8,128)(2,1)}, u32[]{:S(2)}, u32[]{:S(2)}) %all-to-all-start.2) | async-done | bytes 4194336 | tf_op jit(solution)/shard_map/all_to_all | solution.py:194
  112.3 8.7 %collective-permute-start.1 = (bf16[8,16,64,256]{3,2,1,0:T(8,128)(2,1)}, bf16[8,16,64,256]{3,2,1,0:T(8,128)(2,1)}, u32[]{:S(2)}, u32[]{:S(2)}) collective-permute-start(bf16[8,16,64,256]{3,2,1,0:T(8,128)(2,1)} %all-to-all-done.2.near), channel_id=1, source_target_pairs={{0,1},{1,0},{2,3},{3,2},{4,5},{5,4},{6,7},{7,6},{8,9},{9,8},{10,11... | collective-permute-start | bytes 12582920 | tf_op jit(solution)/shard_map/ppermute | solution.py:14
  121.1 3.6 %all-to-all-start.1 = ((bf16[8,256,256]{2,1,0:T(8,128)(2,1)}), bf16[8,256,256]{2,1,0:T(8,128)(2,1)S(1)}, u32[]{:S(2)}, u32[]{:S(2)}) async-start(bf16[8,256,256]{2,1,0:T(8,128)(2,1)} %shard_map.109), calls=%async_computation.1 | async-start | bytes 2097152 | tf_op jit(solution)/shard_map/all_to_all | solution.py:194
  124.6 0.1 pad_add_fusion.place
  124.7 15.8 %all-to-all-done.1.attns = bf16[8,256,256]{2,1,0:T(8,128)(2,1)S(1)} async-done(((bf16[8,256,256]{2,1,0:T(8,128)(2,1)}), bf16[8,256,256]{2,1,0:T(8,128)(2,1)S(1)}, u32[]{:S(2)}, u32[]{:S(2)}) %all-to-all-start.1) | async-done | bytes 1048608 | tf_op jit(solution)/shard_map/all_to_all | solution.py:194
  140.5 0.0 collective-permute-done.1.far
  140.5 0.0 copy-done.1
  140.5 9.8 %shard_map.110 = (bf16[8,256,256]{2,1,0:T(8,128)(2,1)S(1)}, bf16[256,256]{1,0:T(8,128)(2,1)S(1)}) custom-call(s32[2]{0:T(128)S(1)} %pad_add_fusion.place, bf16[8,256,256]{2,1,0:T(8,128)(2,1)S(1)} %all-to-all-done.1.attns, bf16[8,256,256]{2,1,0:T(8,128)(2,1)S(1)} %all-to-all-done.tokens, f32[1,2048]{1,0:T(1,128)S(1)} %bitcast.32, ...), custom_call_target="tpu_custom_call" | custom-call | tf_op jit(solution)/shard_map/pallas_call | solution.py:159
  150.3 17.4 %all_to_all.20 = bf16[8,256,256]{2,1,0:T(8,128)(2,1)S(1)} all-to-all(bf16[8,256,256]{2,1,0:T(8,128)(2,1)S(1)} %get-tuple-element.16), channel_id=1, replica_groups=mesh['rep'=2,'row'=8,'z'=16,'core'=2] {'row'}, dimensions={0} | all-to-all | bytes 2097152 | tf_op jit(solution)/shard_map/all_to_all | solution.py:194
  167.7 0.1 convert_reduce_fusion.1
  167.9 0.7 fusion.2
  (21 shorter events, 0.1 us)
Async XLA Ops:
  6.5 62.8 %copy-start = (s32[2,1]{0,1:T(1,128)S(1)}, s32[2,1]{0,1:T(1,128)}, u32[]{:S(2)}) copy-start(s32[2,1]{0,1:T(1,128)} %param.20) | copy-start | bytes 28
  6.5 96.6 %all-gather.3.cloned.1.call-start = ((), (), s32[]{:S(2)}) async-start(), calls=%async_computation.4 | async-start | bytes 11894784 | tf_op jit(solution)/shard_map/all_gather | solution.py:223
  7.5 13.5 %copy-start.10 = (bf16[256,64]{0,1:T(8,128)(2,1)S(1)}, bf16[256,64]{0,1:T(8,128)(2,1)}, u32[]{:S(2)}) copy-start(bf16[256,64]{0,1:T(8,128)(2,1)} %param.13) | copy-start | bytes 98308
  9.2 50.1 %collective-permute-start = (bf16[1,2,8,128,256]{4,3,2,1,0:T(8,128)(2,1)}, bf16[1,2,8,128,256]{4,3,2,1,0:T(8,128)(2,1)S(1)}, u32[]{:S(2)}, u32[]{:S(2)}) collective-permute-start(bf16[1,2,8,128,256]{4,3,2,1,0:T(8,128)(2,1)} %param.18), channel_id=1, source_target_pairs={{0,256},{256,0},{1,257},{257,1},{2,258},{258,2},{3,259},{259,3},{4... | collective-permute-start | bytes 3145736 | tf_op jit(solution)/shard_map/ppermute | solution.py:14
  16.7 42.7 %all-to-all-start = ((bf16[8,256,256]{2,1,0:T(8,128)(2,1)}), bf16[8,256,256]{2,1,0:T(8,128)(2,1)S(1)}, u32[]{:S(2)}, u32[]{:S(2)}) async-start(bf16[8,256,256]{2,1,0:T(8,128)(2,1)} %broadcast_in_dim.7), calls=%async_computation | async-start | bytes 2097152 | tf_op jit(solution)/shard_map/all_to_all | solution.py:194
  59.4 1.0 copy-start.8
  62.9 7.1 %copy-start.12 = (s32[2,1,8]{2,1,0:T(1,128)S(1)}, s32[2,1,8]{2,1,0:T(1,128)}, u32[]{:S(2)}) copy-start(s32[2,1,8]{2,1,0:T(1,128)} %param.19) | copy-start | bytes 196
  62.9 7.2 %copy-start.7 = (bf16[1,2,8,128,256]{4,3,2,1,0:T(8,128)(2,1)S(1)}, bf16[1,2,8,128,256]{4,3,2,1,0:T(8,128)(2,1)}, u32[]{:S(2)}) copy-start(bf16[1,2,8,128,256]{4,3,2,1,0:T(8,128)(2,1)} %param.18) | copy-start | bytes 3145732
  62.9 49.5 %all-to-all-start.2 = ((bf16[8,16,64,256]{3,2,1,0:T(8,128)(2,1)}), bf16[8,16,64,256]{3,2,1,0:T(8,128)(2,1)}, u32[]{:S(2)}, u32[]{:S(2)}) async-start(bf16[8,16,64,256]{3,2,1,0:T(8,128)(2,1)} %broadcast_in_dim.8), calls=%async_computation.2 | async-start | bytes 8388608 | tf_op jit(solution)/shard_map/all_to_all | solution.py:194
  70.1 2.8 %copy-start.9 = (bf16[1,2,8,128,256]{4,3,2,1,0:T(8,128)(2,1)S(1)}, bf16[1,2,8,128,256]{4,3,2,1,0:T(8,128)(2,1)}, u32[]{:S(2)}) copy-start(bf16[1,2,8,128,256]{4,3,2,1,0:T(8,128)(2,1)} %copy-done.8) | copy-start | bytes 3145732
  81.1 1.0 copy-start.3
  81.1 1.2 copy-start.4
  81.2 1.4 copy-start.5
  81.2 1.6 copy-start.6
  81.4 2.1 %copy-start.2 = (f32[256,2048]{1,0:T(8,128)S(1)}, f32[256,2048]{1,0:T(8,128)}, u32[]{:S(2)}) copy-start(f32[256,2048]{1,0:T(8,128)} %copy.14) | copy-start | bytes 6291460
  81.4 2.1 %copy-start.11 = (f32[2048]{0:T(1024)S(1)}, f32[2048]{0:T(1024)}, u32[]{:S(2)}) copy-start(f32[2048]{0:T(1024)} %param.16) | copy-start | bytes 24580
  110.5 30.0 %copy-start.1 = (f32[2048]{0:T(1024)S(1)}, f32[2048]{0:T(1024)}, u32[]{:S(2)}) copy-start(f32[2048]{0:T(1024)} %param.17) | copy-start | bytes 24580
  112.3 28.1 %collective-permute-start.1 = (bf16[8,16,64,256]{3,2,1,0:T(8,128)(2,1)}, bf16[8,16,64,256]{3,2,1,0:T(8,128)(2,1)}, u32[]{:S(2)}, u32[]{:S(2)}) collective-permute-start(bf16[8,16,64,256]{3,2,1,0:T(8,128)(2,1)} %all-to-all-done.2.near), channel_id=1, source_target_pairs={{0,1},{1,0},{2,3},{3,2},{4,5},{5,4},{6,7},{7,6},{8,9},{9,8},{10,11... | collective-permute-start | bytes 12582920 | tf_op jit(solution)/shard_map/ppermute | solution.py:14
  121.1 19.4 %all-to-all-start.1 = ((bf16[8,256,256]{2,1,0:T(8,128)(2,1)}), bf16[8,256,256]{2,1,0:T(8,128)(2,1)S(1)}, u32[]{:S(2)}, u32[]{:S(2)}) async-start(bf16[8,256,256]{2,1,0:T(8,128)(2,1)} %shard_map.109), calls=%async_computation.1 | async-start | bytes 2097152 | tf_op jit(solution)/shard_map/all_to_all | solution.py:194
Sparse Core Ops, SparseCore 0:
  9.5 93.5 all-gather.2

commit v4 on v3

--- a/solution.py
+++ b/solution.py
@@ -1,3 +1,5 @@
+import math
+
 import jax
 import jax.numpy as jnp
 from jax import lax
@@ -8,6 +10,7 @@
 
 D = 2048
 H = 16
+GROUPS = 4
 
 
 def swapped(value, axis, apart):
@@ -40,7 +43,8 @@
         cached = keys.shape[0]
         share = keys.shape[1]
         head_width = D // H
-        scale = jnp.float32(head_width) ** -0.5
+        fold = jnp.float32(math.log2(math.e))
+        scale = fold * jnp.float32(head_width) ** -0.5
         cache_pos = lax.broadcasted_iota(jnp.int32, (1, cached), 1)
         cache_ok = cache_pos < length
         cache_off = (cache_pos - length).astype(jnp.float32)
@@ -55,17 +59,17 @@
                 return total[:, start : start + head_width].astype(jnp.bfloat16)
 
             query, new_key, new_value = part(0), part(1), part(2)
-            slope = slopes[head]
-            cache_score = times_transposed(query, keys[:, lanes]) * scale
-            cache_score = jnp.where(cache_ok, cache_score + slope * cache_off, -1e30)
-            new_score = times_transposed(query, new_key) * scale
-            new_score = jnp.where(new_ok, new_score + slope * new_off, -1e30)
+            slope = fold * slopes[head]
+            cache_bias = jnp.where(cache_ok, slope * cache_off, -1e30)
+            cache_score = times_transposed(query, keys[:, lanes]) * scale + cache_bias
+            new_score = times_transposed(query, new_key) * scale + slope * new_off
+            new_score = jnp.where(new_ok, new_score, -1e30)
             top = jnp.maximum(
                 jnp.max(cache_score, axis=1, keepdims=True),
                 jnp.max(new_score, axis=1, keepdims=True),
             )
-            cache_weight = jnp.exp(cache_score - top)
-            new_weight = jnp.exp(new_score - top)
+            cache_weight = jnp.exp2(cache_score - top)
+            new_weight = jnp.exp2(new_score - top)
             whole = jnp.sum(cache_weight, axis=1, keepdims=True) + jnp.sum(
                 new_weight, axis=1, keepdims=True
             )
@@ -80,7 +84,7 @@
 def attend(normed, weights, keys, values, length, slopes, rows):
     seq, width = normed.shape
     share = keys.shape[1]
-    steps = 4
+    steps = 2
     deep = width // steps
     return pl.pallas_call(
         attend_kernel,
@@ -117,18 +121,23 @@
         copies.append(pltpu.make_async_copy(source, target, sems.at[len(copies)]))
         copies[-1].start()
 
-    for row in range(rows):
-        lanes = pl.ds(row * share, share)
-        copy(near.at[row], out_weights.at[:, place[0], :, lanes])
-        copy(far.at[row], out_weights.at[:, 1 - place[0], :, lanes])
+    span = chips // GROUPS
+    for group in range(GROUPS):
+        picked = pl.ds(group * span, span)
+        for row in range(rows):
+            lanes = pl.ds(row * share, share)
+            copy(near.at[row, picked], out_weights.at[picked, place[0], :, lanes])
+            copy(far.at[row, picked], out_weights.at[picked, 1 - place[0], :, lanes])
     for part in range(2):
         copy(gathered.at[:, pl.ds(first + part * hidden_share, hidden_share)], feed_weights.at[part])
     for row in range(rows):
         wide[:, row * share : (row + 1) * share] = attns[row]
-    for item in copies[: 2 * rows]:
-        item.wait()
     each = chips // rows
     for row in range(rows):
+        if row % (rows // GROUPS) == 0:
+            group = row // (rows // GROUPS)
+            for item in copies[2 * rows * group : 2 * rows * (group + 1)]:
+                item.wait()
         block = out_weights[row * each : (row + 1) * each].reshape(share, width)
         mixed = times_transposed(wide[...], block)
         state[row] = (tokens[row].astype(jnp.float32) + mixed).astype(jnp.bfloat16)
@@ -141,12 +150,12 @@
     for row in range(rows):
         lanes = slice(row * share, (row + 1) * share)
         wide[:, lanes] = (centred[row] * factor * gain[:, lanes]).astype(jnp.bfloat16)
-    copies[2 * rows].wait()
+    copies[-2].wait()
     for part in range(4):
         lanes = slice(part * hidden_share // 4, (part + 1) * hidden_share // 4)
         up = jnp.dot(wide[...], feed_weights[0, :, lanes], preferred_element_type=jnp.float32)
         hidden[:, lanes] = jax.nn.gelu(up, approximate=True).astype(jnp.bfloat16)
-    copies[2 * rows + 1].wait()
+    copies[-1].wait()
     for row in range(rows):
         lanes = slice(row * share, (row + 1) * share)
         down[row] = times_transposed(hidden[...], feed_weights[1, lanes, :]).astype(jnp.bfloat16)
@@ -183,11 +192,27 @@
                 pltpu.VMEM((seq, width), jnp.bfloat16),
                 pltpu.VMEM(attns.shape, jnp.bfloat16),
                 pltpu.VMEM((seq, hidden_share), jnp.bfloat16),
-                pltpu.SemaphoreType.DMA((2 * rows + 2,)),
+                pltpu.SemaphoreType.DMA((2 * rows * GROUPS + 2,)),
             ],
         ),
         compiler_params=pltpu.CompilerParams(vmem_limit_bytes=48 << 20),
     )(place, attns, tokens, gain.reshape(1, width), near, far, gathered)
+
+
+def pack_kernel(qkv, up, down, shard):
+    start = 0
+    for source in [qkv.at[part] for part in range(qkv.shape[0])] + [up, down]:
+        shard[:, start : start + source.shape[1]] = source[...]
+        start += source.shape[1]
+
+
+def pack(qkv, up, down):
+    parts, rows, share = qkv.shape
+    width = parts * share + up.shape[1] + down.shape[1]
+    return pl.pallas_call(
+        pack_kernel,
+        out_shape=jax.ShapeDtypeStruct((rows, width), jnp.bfloat16),
+    )(qkv, up, down)
 
 
 def row_exchange(parts):
@@ -219,7 +244,7 @@
     heads = share // head_width
     inputs = tokens.reshape(seq, share)
     spread_tokens = row_gather(inputs)
-    shard = jnp.concatenate([w_qkv.reshape(w_qkv.shape[0], -1), w_up, w_down.T], axis=1)
+    shard = pack(jnp.swapaxes(w_qkv, 0, 1), w_up, w_down.T)
     weights = lax.all_gather(shard, ("z", "core"), axis=0, tiled=True)
     other = swapped(kv_pool, "rep", 0)
     out_block = lax.all_gather(w_out.T, "z", axis=0, tiled=False)

time: 176 us -> 172 us (0.977)
    all_gather x1, waiting for transfers between devices: 19.2 us -> 22.3 us  [local(): weights = lax.all_gather(shard, ('z', 'core'), axis=0, tiled=True)]
    all_to_all x3, waiting for transfers between devices: 17.6 us -> 15.8 us  [row_exchange(): return lax.all_to_all(parts, 'row', 0, 0, tiled=True)]
    pallas_call x0 -> x1, Pallas kernels: none -> 1.79 us  [pack(): pl.pallas_call(pack_kernel, out_shape=jax.ShapeDtypeStruct((rows, width),...]
  transfers between devices with their start and end apart: 6 -> 6, of which waited for: 3 -> 2; matrix products, arithmetic and copies ran while one was open for 10% -> 10% of each run, Pallas kernels for 4% -> 4%
where the time goes in v4:
time: 172 us
  blocking collectives  54.6 us (32%)
  waiting for transfers between devices  38.1 us (22%)
  starting transfers between devices  26.5 us (15%)
  local copies, waits for them, and re-layouts  17.3 us (10%)
  Pallas kernels  17.2 us (10%)
  between operations  14.2 us (8%)
  other arithmetic  3.6 us (2%)
    all_gather x1, blocking collectives, local(): out_block = lax.all_gather(w_out.T, 'z', axis=0, tiled=False)  37.2 us
    all_gather x1, waiting for transfers between devices, local(): weights = lax.all_gather(shard, ('z', 'core'), axis=0, tiled=True)  22.3 us
    all_to_all x1, blocking collectives, row_exchange(): return lax.all_to_all(parts, 'row', 0, 0, tiled=True)  17.4 us
    all_to_all x3, waiting for transfers between devices, row_exchange(): return lax.all_to_all(parts, 'row', 0, 0, tiled=True)  15.8 us
    ppermute x2, starting transfers between devices, swapped(): lax.ppermute(value, axis, [(i, i ^ 1 << apart) for i in range(lax.axis_si...  13.9 us
    all_to_all x3, starting transfers between devices, row_exchange(): return lax.all_to_all(parts, 'row', 0, 0, tiled=True)  12.6 us
    pallas_call x1, Pallas kernels, feed(): pl.pallas_call(feed_kernel, out_shape=(jax.ShapeDtypeStruct(attns.shape,...  9.08 us
    pallas_call x1, Pallas kernels, attend(): pl.pallas_call(attend_kernel, out_shape=jax.ShapeDtypeStruct((rows, seq,...  6.33 us
  transfers between devices with their start and end apart: 6, of which 2 were waited for; matrix products, arithmetic and copies ran while one was open for 10% of the time, Pallas kernels for 4%

profile of v4, /device:TPU:1, one launch (start us, length us, event | category | flops | bytes accessed | tf_op | source)
XLA Modules:
  0.0 171.6 jit_solution(7378850562627666245)
XLA Ops:
  6.5 0.0 copy-start
  6.5 0.0 all-gather.3.cloned.1.call-start
  6.5 1.8 %shard_map.109 = bf16[64,2816]{1,0:T(8,128)(2,1)} custom-call(bf16[3,64,256]{2,1,0:T(8,128)(2,1)} %bitcast.36, bf16[64,1024]{1,0:T(8,128)(2,1)} %up.1, bf16[64,1024]{1,0:T(8,128)(2,1)} %bitcast.35), custom_call_target="tpu_custom_call" | custom-call | tf_op jit(solution)/shard_map/pallas_call | solution.py:212
  8.3 0.0 all-gather.3.cloned.1.call-update
  8.4 5.5 %collective-permute-start = (bf16[1,2,8,128,256]{4,3,2,1,0:T(8,128)(2,1)}, bf16[1,2,8,128,256]{4,3,2,1,0:T(8,128)(2,1)S(1)}, u32[]{:S(2)}, u32[]{:S(2)}) collective-permute-start(bf16[1,2,8,128,256]{4,3,2,1,0:T(8,128)(2,1)} %param.18), channel_id=1, source_target_pairs={{0,256},{256,0},{1,257},{257,1},{2,258},{258,2},{3,259},{259,3},{4... | collective-permute-start | bytes 3145736 | tf_op jit(solution)/shard_map/ppermute | solution.py:17
  13.8 2.0 %broadcast_in_dim.7 = bf16[8,256,256]{2,1,0:T(8,128)(2,1)} broadcast(bf16[256,256]{1,0:T(8,128)(2,1)} %bitcast.34), dimensions={1,2} | broadcast | bytes 1179648 | tf_op jit(solution)/shard_map/broadcast_in_dim | solution.py:223
  15.8 4.2 %all-to-all-start = ((bf16[8,256,256]{2,1,0:T(8,128)(2,1)}), bf16[8,256,256]{2,1,0:T(8,128)(2,1)S(1)}, u32[]{:S(2)}, u32[]{:S(2)}) async-start(bf16[8,256,256]{2,1,0:T(8,128)(2,1)} %broadcast_in_dim.7), calls=%async_computation | async-start | bytes 2097152 | tf_op jit(solution)/shard_map/all_to_all | solution.py:219
  20.0 0.0 copy-done.10
  20.1 37.2 %all-gather = bf16[1024,256]{1,0:T(8,128)(2,1)S(1)} all-gather(bf16[64,256]{1,0:T(8,128)(2,1)S(1)} %bitcast.37), channel_id=2, replica_groups=mesh['rep'=2,'row'=8,'z'=16,'core'=2] {'z'}, dimensions={0}, use_global_device_ids=true | all-gather | bytes 557056 | tf_op jit(solution)/shard_map/all_gather | solution.py:250
  57.2 0.0 all-to-all-done.tokens
  57.2 0.0 collective-permute-done
  57.3 1.0 copy-done.8
  58.2 2.5 %broadcast_in_dim.8 = bf16[8,16,64,256]{3,2,1,0:T(8,128)(2,1)} broadcast(bf16[16,64,256]{2,1,0:T(8,128)(2,1)S(1)} %bitcast.33), dimensions={1,2,3} | broadcast | bytes 4718592 | tf_op jit(solution)/shard_map/broadcast_in_dim | solution.py:223
  60.8 4.8 %all-to-all-start.2 = ((bf16[8,16,64,256]{3,2,1,0:T(8,128)(2,1)}), bf16[8,16,64,256]{3,2,1,0:T(8,128)(2,1)}, u32[]{:S(2)}, u32[]{:S(2)}) async-start(bf16[8,16,64,256]{3,2,1,0:T(8,128)(2,1)} %broadcast_in_dim.8), calls=%async_computation.2 | async-start | bytes 8388608 | tf_op jit(solution)/shard_map/all_to_all | solution.py:219
  66.2 0.0 copy-done
  66.2 0.7 constant_dynamic-slice_fusion
  66.9 0.0 copy-done.12
  66.9 0.1 slice_bitcast_fusion
  67.0 1.4 gather_fusion.3
  68.4 1.4 gather_fusion.1
  69.8 0.1 slice_bitcast_fusion.1
  69.9 1.4 gather_fusion.2
  71.3 1.4 gather_fusion
  72.7 1.5 convert_bitcast_fusion
  74.2 2.0 %copy.12 = f32[256,8,256]{0,2,1:T(8,128)S(1)} copy(f32[256,8,256]{2,0,1:T(8,128)} %convert_bitcast_fusion) | data formatting | bytes 4194304 | tf_op jit(solution)/shard_map/convert_element_type | solution.py:254
  76.2 1.9 %copy.13 = f32[256,2048]{1,0:T(8,128)} copy(f32[256,2048]{0,1:T(8,128)S(1)} %bitcast.32) | data formatting | bytes 4194304 | tf_op jit(solution)/shard_map/convert_element_type | solution.py:254
  78.1 0.2 convert_reduce_fusion
  78.3 0.0 copy-start.11
  78.3 0.4 fusion.1
  78.7 0.4 copy-done.3
  79.1 0.2 copy-done.4
  79.3 0.2 copy-done.5
  79.4 0.2 copy-done.6
  79.6 0.1 broadcast_select_fusion
  79.7 0.7 copy-done.2
  80.4 0.4 multiply_convert_fusion.normed
  80.8 22.3 %all-gather.3.cloned.1.call-done.weights.gathered = bf16[2048,2816]{1,0:T(8,128)(2,1)} async-done(((bf16[64,2816]{1,0:T(8,128)(2,1)}), bf16[2048,2816]{1,0:T(8,128)(2,1)}) %all-gather.3.cloned.1.call-update) | async-done | bytes 11534352 | tf_op jit(solution)/shard_map/all_gather | solution.py:248
  103.2 6.3 %shard_map.110 = bf16[8,256,256]{2,1,0:T(8,128)(2,1)} custom-call(s32[1]{0:T(128)} %bitcast.3.scalars, f32[2]{0:T(128)S(1)} %multiply_power_fusion.slopes, bf16[256,2048]{1,0:T(8,128)(2,1)S(1)} %multiply_convert_fusion.normed, bf16[2048,2816]{1,0:T(8,128)(2,1)} %all-gather.3.cloned.1.call-done.weights.gathered, bf16[1024,256]{1,0:T(8,128)(2,1)S(1)} %bitcast.30, ...), custom_call_target="tpu_custom_call" | custom-call | tf_op jit(solution)/shard_map/pallas_call | solution.py:89
  109.5 0.0 all-to-all-done.2.near
  109.5 8.5 %collective-permute-start.1 = (bf16[8,16,64,256]{3,2,1,0:T(8,128)(2,1)}, bf16[8,16,64,256]{3,2,1,0:T(8,128)(2,1)}, u32[]{:S(2)}, u32[]{:S(2)}) collective-permute-start(bf16[8,16,64,256]{3,2,1,0:T(8,128)(2,1)} %all-to-all-done.2.near), channel_id=1, source_target_pairs={{0,1},{1,0},{2,3},{3,2},{4,5},{5,4},{6,7},{7,6},{8,9},{9,8},{10,11... | collective-permute-start | bytes 12582920 | tf_op jit(solution)/shard_map/ppermute | solution.py:17
  118.0 3.6 %all-to-all-start.1 = ((bf16[8,256,256]{2,1,0:T(8,128)(2,1)}), bf16[8,256,256]{2,1,0:T(8,128)(2,1)S(1)}, u32[]{:S(2)}, u32[]{:S(2)}) async-start(bf16[8,256,256]{2,1,0:T(8,128)(2,1)} %shard_map.110), calls=%async_computation.1 | async-start | bytes 2097152 | tf_op jit(solution)/shard_map/all_to_all | solution.py:219
  121.6 0.1 pad_add_fusion.place
  121.6 15.8 %all-to-all-done.1.attns = bf16[8,256,256]{2,1,0:T(8,128)(2,1)S(1)} async-done(((bf16[8,256,256]{2,1,0:T(8,128)(2,1)}), bf16[8,256,256]{2,1,0:T(8,128)(2,1)S(1)}, u32[]{:S(2)}, u32[]{:S(2)}) %all-to-all-start.1) | async-done | bytes 1048608 | tf_op jit(solution)/shard_map/all_to_all | solution.py:219
  137.4 0.0 collective-permute-done.1.far
  137.4 9.1 %shard_map.111 = (bf16[8,256,256]{2,1,0:T(8,128)(2,1)S(1)}, bf16[256,256]{1,0:T(8,128)(2,1)S(1)}) custom-call(s32[2]{0:T(128)S(1)} %pad_add_fusion.place, bf16[8,256,256]{2,1,0:T(8,128)(2,1)S(1)} %all-to-all-done.1.attns, bf16[8,256,256]{2,1,0:T(8,128)(2,1)S(1)} %all-to-all-done.tokens, f32[1,2048]{1,0:T(1,128)S(1)} %bitcast.31, ...), custom_call_target="tpu_custom_call" | custom-call | tf_op jit(solution)/shard_map/pallas_call | solution.py:168
  146.5 17.4 %all_to_all.20 = bf16[8,256,256]{2,1,0:T(8,128)(2,1)S(1)} all-to-all(bf16[8,256,256]{2,1,0:T(8,128)(2,1)S(1)} %get-tuple-element.16), channel_id=1, replica_groups=mesh['rep'=2,'row'=8,'z'=16,'core'=2] {'row'}, dimensions={0} | all-to-all | bytes 2097152 | tf_op jit(solution)/shard_map/all_to_all | solution.py:219
  163.9 0.1 convert_reduce_fusion.1
  164.0 0.7 fusion.2
  (20 shorter events, 0.1 us)
Async XLA Ops:
  6.5 59.7 %copy-start = (s32[2,1]{0,1:T(1,128)S(1)}, s32[2,1]{0,1:T(1,128)}, u32[]{:S(2)}) copy-start(s32[2,1]{0,1:T(1,128)} %param.20) | copy-start | bytes 28
  6.5 96.6 %all-gather.3.cloned.1.call-start = ((), (), s32[]{:S(2)}) async-start(), calls=%async_computation.4 | async-start | bytes 11894784 | tf_op jit(solution)/shard_map/all_gather | solution.py:248
  6.5 13.5 %copy-start.10 = (bf16[256,64]{0,1:T(8,128)(2,1)S(1)}, bf16[256,64]{0,1:T(8,128)(2,1)}, u32[]{:S(2)}) copy-start(bf16[256,64]{0,1:T(8,128)(2,1)} %param.13) | copy-start | bytes 98308
  8.4 48.9 %collective-permute-start = (bf16[1,2,8,128,256]{4,3,2,1,0:T(8,128)(2,1)}, bf16[1,2,8,128,256]{4,3,2,1,0:T(8,128)(2,1)S(1)}, u32[]{:S(2)}, u32[]{:S(2)}) collective-permute-start(bf16[1,2,8,128,256]{4,3,2,1,0:T(8,128)(2,1)} %param.18), channel_id=1, source_target_pairs={{0,256},{256,0},{1,257},{257,1},{2,258},{258,2},{3,259},{259,3},{4... | collective-permute-start | bytes 3145736 | tf_op jit(solution)/shard_map/ppermute | solution.py:17
  15.8 41.4 %all-to-all-start = ((bf16[8,256,256]{2,1,0:T(8,128)(2,1)}), bf16[8,256,256]{2,1,0:T(8,128)(2,1)S(1)}, u32[]{:S(2)}, u32[]{:S(2)}) async-start(bf16[8,256,256]{2,1,0:T(8,128)(2,1)} %broadcast_in_dim.7), calls=%async_computation | async-start | bytes 2097152 | tf_op jit(solution)/shard_map/all_to_all | solution.py:219
  57.2 1.0 copy-start.8
  60.8 6.1 %copy-start.12 = (s32[2,1,8]{2,1,0:T(1,128)S(1)}, s32[2,1,8]{2,1,0:T(1,128)}, u32[]{:S(2)}) copy-start(s32[2,1,8]{2,1,0:T(1,128)} %param.19) | copy-start | bytes 196
  60.8 6.1 %copy-start.7 = (bf16[1,2,8,128,256]{4,3,2,1,0:T(8,128)(2,1)S(1)}, bf16[1,2,8,128,256]{4,3,2,1,0:T(8,128)(2,1)}, u32[]{:S(2)}) copy-start(bf16[1,2,8,128,256]{4,3,2,1,0:T(8,128)(2,1)} %param.18) | copy-start | bytes 3145732
  60.8 48.7 %all-to-all-start.2 = ((bf16[8,16,64,256]{3,2,1,0:T(8,128)(2,1)}), bf16[8,16,64,256]{3,2,1,0:T(8,128)(2,1)}, u32[]{:S(2)}, u32[]{:S(2)}) async-start(bf16[8,16,64,256]{3,2,1,0:T(8,128)(2,1)} %broadcast_in_dim.8), calls=%async_computation.2 | async-start | bytes 8388608 | tf_op jit(solution)/shard_map/all_to_all | solution.py:219
  67.0 2.8 %copy-start.9 = (bf16[1,2,8,128,256]{4,3,2,1,0:T(8,128)(2,1)S(1)}, bf16[1,2,8,128,256]{4,3,2,1,0:T(8,128)(2,1)}, u32[]{:S(2)}) copy-start(bf16[1,2,8,128,256]{4,3,2,1,0:T(8,128)(2,1)} %copy-done.8) | copy-start | bytes 3145732
  78.0 1.1 copy-start.3
  78.0 1.2 copy-start.4
  78.0 1.4 copy-start.5
  78.1 1.6 copy-start.6
  78.3 2.2 %copy-start.2 = (f32[256,2048]{1,0:T(8,128)S(1)}, f32[256,2048]{1,0:T(8,128)}, u32[]{:S(2)}) copy-start(f32[256,2048]{1,0:T(8,128)} %copy.13) | copy-start | bytes 6291460
  78.3 2.1 %copy-start.11 = (f32[2048]{0:T(1024)S(1)}, f32[2048]{0:T(1024)}, u32[]{:S(2)}) copy-start(f32[2048]{0:T(1024)} %param.16) | copy-start | bytes 24580
  109.5 27.9 %copy-start.1 = (f32[2048]{0:T(1024)S(1)}, f32[2048]{0:T(1024)}, u32[]{:S(2)}) copy-start(f32[2048]{0:T(1024)} %param.17) | copy-start | bytes 24580
  109.5 27.9 %collective-permute-start.1 = (bf16[8,16,64,256]{3,2,1,0:T(8,128)(2,1)}, bf16[8,16,64,256]{3,2,1,0:T(8,128)(2,1)}, u32[]{:S(2)}, u32[]{:S(2)}) collective-permute-start(bf16[8,16,64,256]{3,2,1,0:T(8,128)(2,1)} %all-to-all-done.2.near), channel_id=1, source_target_pairs={{0,1},{1,0},{2,3},{3,2},{4,5},{5,4},{6,7},{7,6},{8,9},{9,8},{10,11... | collective-permute-start | bytes 12582920 | tf_op jit(solution)/shard_map/ppermute | solution.py:17
  118.0 19.4 %all-to-all-start.1 = ((bf16[8,256,256]{2,1,0:T(8,128)(2,1)}), bf16[8,256,256]{2,1,0:T(8,128)(2,1)S(1)}, u32[]{:S(2)}, u32[]{:S(2)}) async-start(bf16[8,256,256]{2,1,0:T(8,128)(2,1)} %shard_map.110), calls=%async_computation.1 | async-start | bytes 2097152 | tf_op jit(solution)/shard_map/all_to_all | solution.py:219
Sparse Core Ops, SparseCore 0:
  9.5 93.6 all-gather.2

commit v5 on v4

--- a/solution.py
+++ b/solution.py
@@ -199,20 +199,34 @@
     )(place, attns, tokens, gain.reshape(1, width), near, far, gathered)
 
 
-def pack_kernel(qkv, up, down, shard):
+def pack_kernel(qkv, up, down, tokens, shard, copies, sems):
+    moves = [
+        pltpu.make_async_copy(tokens, copies.at[row], sems.at[row]) for row in range(copies.shape[0])
+    ]
+    for move in moves:
+        move.start()
     start = 0
     for source in [qkv.at[part] for part in range(qkv.shape[0])] + [up, down]:
         shard[:, start : start + source.shape[1]] = source[...]
         start += source.shape[1]
-
-
-def pack(qkv, up, down):
+    for move in moves:
+        move.wait()
+
+
+def pack(qkv, up, down, tokens, size):
     parts, rows, share = qkv.shape
     width = parts * share + up.shape[1] + down.shape[1]
+    on_chip = pl.BlockSpec(memory_space=pltpu.VMEM)
     return pl.pallas_call(
         pack_kernel,
-        out_shape=jax.ShapeDtypeStruct((rows, width), jnp.bfloat16),
-    )(qkv, up, down)
+        out_shape=(
+            jax.ShapeDtypeStruct((rows, width), jnp.bfloat16),
+            jax.ShapeDtypeStruct((size,) + tokens.shape, jnp.bfloat16),
+        ),
+        in_specs=[on_chip] * 4,
+        out_specs=(on_chip, pl.BlockSpec(memory_space=pl.ANY)),
+        scratch_shapes=[pltpu.SemaphoreType.DMA((size,))],
+    )(qkv, up, down, tokens)
 
 
 def row_exchange(parts):
@@ -243,8 +257,10 @@
     head_width = D // H
     heads = share // head_width
     inputs = tokens.reshape(seq, share)
-    spread_tokens = row_gather(inputs)
-    shard = pack(jnp.swapaxes(w_qkv, 0, 1), w_up, w_down.T)
+    shard, token_copies = pack(
+        jnp.swapaxes(w_qkv, 0, 1), w_up, w_down.T, inputs, lax.axis_size("row")
+    )
+    spread_tokens = row_exchange(token_copies)
     weights = lax.all_gather(shard, ("z", "core"), axis=0, tiled=True)
     other = swapped(kv_pool, "rep", 0)
     out_block = lax.all_gather(w_out.T, "z", axis=0, tiled=False)

time: 172 us -> 173 us (level)
  local copies, waits for them, and re-layouts: 17.3 us -> 15.3 us
    broadcast_in_dim x2 -> x1, local copies, waits for them, and re-layouts: 4.49 us -> 2.52 us  [row_gather(): jnp.broadcast_to(value[None], (lax.axis_size('row'),) + value.shape)]
  transfers between devices with their start and end apart: 6 -> 6, of which waited for: 2 -> 2; matrix products, arithmetic and copies ran while one was open for 10% -> 9% of each run, Pallas kernels for 4% -> 4%
where the time goes in v5:
time: 173 us; the launch traced here: 172 us
  blocking collectives  55.5 us (32%)
  waiting for transfers between devices  38.1 us (22%)
  starting transfers between devices  26.4 us (15%)
  Pallas kernels  18.3 us (11%)
  local copies, waits for them, and re-layouts  15.3 us (9%)
  between operations  14.2 us (8%)
  other arithmetic  3.6 us (2%)
    all_gather x1, blocking collectives, local(): out_block = lax.all_gather(w_out.T, 'z', axis=0, tiled=False)  38.1 us
    all_gather x1, waiting for transfers between devices, local(): weights = lax.all_gather(shard, ('z', 'core'), axis=0, tiled=True)  22.3 us
    all_to_all x1, blocking collectives, row_exchange(): return lax.all_to_all(parts, 'row', 0, 0, tiled=True)  17.4 us
    all_to_all x3, waiting for transfers between devices, row_exchange(): return lax.all_to_all(parts, 'row', 0, 0, tiled=True)  15.8 us
    ppermute x2, starting transfers between devices, swapped(): lax.ppermute(value, axis, [(i, i ^ 1 << apart) for i in range(lax.axis_si...  14 us
    all_to_all x3, starting transfers between devices, row_exchange(): return lax.all_to_all(parts, 'row', 0, 0, tiled=True)  12.5 us
    pallas_call x1, Pallas kernels, feed(): pl.pallas_call(feed_kernel, out_shape=(jax.ShapeDtypeStruct(attns.shape,...  9.08 us
    pallas_call x1, Pallas kernels, attend(): pl.pallas_call(attend_kernel, out_shape=jax.ShapeDtypeStruct((rows, seq,...  6.33 us
  transfers between devices with their start and end apart: 6, of which 2 were waited for; matrix products, arithmetic and copies ran while one was open for 9% of the time, Pallas kernels for 4%

profile of v5, /device:TPU:1, one launch (start us, length us, event | category | flops | bytes accessed | tf_op | source)
XLA Modules:
  0.0 171.5 jit_solution(12254905451186748038)
XLA Ops:
  6.5 0.0 copy-start
  6.5 0.0 all-gather.3.cloned.1.call-start
  6.5 2.9 %shard_map.109 = (bf16[64,2816]{1,0:T(8,128)(2,1)}, bf16[8,256,256]{2,1,0:T(8,128)(2,1)}) custom-call(bf16[3,64,256]{2,1,0:T(8,128)(2,1)} %bitcast.36, bf16[64,1024]{1,0:T(8,128)(2,1)} %up.1, bf16[64,1024]{1,0:T(8,128)(2,1)} %bitcast.34, bf16[256,256]{1,0:T(8,128)(2,1)} %bitcast.35), custom_call_target="tpu_custom_call" | custom-call | tf_op jit(solution)/shard_map/pallas_call | solution.py:220
  9.5 0.0 all-gather.3.cloned.1.call-update
  9.5 5.5 %collective-permute-start = (bf16[1,2,8,128,256]{4,3,2,1,0:T(8,128)(2,1)}, bf16[1,2,8,128,256]{4,3,2,1,0:T(8,128)(2,1)S(1)}, u32[]{:S(2)}, u32[]{:S(2)}) collective-permute-start(bf16[1,2,8,128,256]{4,3,2,1,0:T(8,128)(2,1)} %param.18), channel_id=1, source_target_pairs={{0,256},{256,0},{1,257},{257,1},{2,258},{258,2},{3,259},{259,3},{4... | collective-permute-start | bytes 3145736 | tf_op jit(solution)/shard_map/ppermute | solution.py:17
  15.0 4.2 %all-to-all-start = ((bf16[8,256,256]{2,1,0:T(8,128)(2,1)}), bf16[8,256,256]{2,1,0:T(8,128)(2,1)S(1)}, u32[]{:S(2)}, u32[]{:S(2)}) async-start(bf16[8,256,256]{2,1,0:T(8,128)(2,1)} %get-tuple-element.13), calls=%async_computation | async-start | bytes 2097152 | tf_op jit(solution)/shard_map/all_to_all | solution.py:233
  19.2 0.0 copy-done.10
  19.2 38.1 %all-gather = bf16[1024,256]{1,0:T(8,128)(2,1)S(1)} all-gather(bf16[64,256]{1,0:T(8,128)(2,1)S(1)} %bitcast.37), channel_id=2, replica_groups=mesh['rep'=2,'row'=8,'z'=16,'core'=2] {'z'}, dimensions={0}, use_global_device_ids=true | all-gather | bytes 557056 | tf_op jit(solution)/shard_map/all_gather | solution.py:266
  57.4 0.0 all-to-all-done.tokens
  57.4 0.0 collective-permute-done
  57.4 1.0 copy-done.8
  58.4 2.5 %broadcast_in_dim.2 = bf16[8,16,64,256]{3,2,1,0:T(8,128)(2,1)} broadcast(bf16[16,64,256]{2,1,0:T(8,128)(2,1)S(1)} %bitcast.33), dimensions={1,2,3} | broadcast | bytes 4718592 | tf_op jit(solution)/shard_map/broadcast_in_dim | solution.py:237
  60.9 4.7 %all-to-all-start.2 = ((bf16[8,16,64,256]{3,2,1,0:T(8,128)(2,1)}), bf16[8,16,64,256]{3,2,1,0:T(8,128)(2,1)}, u32[]{:S(2)}, u32[]{:S(2)}) async-start(bf16[8,16,64,256]{3,2,1,0:T(8,128)(2,1)} %broadcast_in_dim.2), calls=%async_computation.2 | async-start | bytes 8388608 | tf_op jit(solution)/shard_map/all_to_all | solution.py:233
  66.2 0.0 copy-done
  66.3 0.6 constant_dynamic-slice_fusion
  66.9 0.0 copy-done.12
  66.9 0.0 copy-done.7
  66.9 0.1 slice_bitcast_fusion
  67.0 1.4 gather_fusion.3
  68.4 1.4 gather_fusion.1
  69.8 0.1 slice_bitcast_fusion.1
  69.9 1.4 gather_fusion.2
  71.3 1.4 gather_fusion
  72.6 1.5 convert_bitcast_fusion
  74.2 2.0 %copy.12 = f32[256,8,256]{0,2,1:T(8,128)S(1)} copy(f32[256,8,256]{2,0,1:T(8,128)} %convert_bitcast_fusion) | data formatting | bytes 4194304 | tf_op jit(solution)/shard_map/convert_element_type | solution.py:270
  76.2 1.9 %copy.13 = f32[256,2048]{1,0:T(8,128)} copy(f32[256,2048]{0,1:T(8,128)S(1)} %bitcast.32) | data formatting | bytes 4194304 | tf_op jit(solution)/shard_map/convert_element_type | solution.py:270
  78.0 0.2 convert_reduce_fusion
  78.3 0.0 copy-start.11
  78.3 0.4 fusion.1
  78.7 0.4 copy-done.3
  79.1 0.2 copy-done.4
  79.2 0.2 copy-done.5
  79.4 0.2 copy-done.6
  79.6 0.1 broadcast_select_fusion
  79.7 0.7 copy-done.2
  80.4 0.4 multiply_convert_fusion.normed
  80.8 22.3 %all-gather.3.cloned.1.call-done.weights.gathered = bf16[2048,2816]{1,0:T(8,128)(2,1)} async-done(((bf16[64,2816]{1,0:T(8,128)(2,1)}), bf16[2048,2816]{1,0:T(8,128)(2,1)}) %all-gather.3.cloned.1.call-update) | async-done | bytes 11534352 | tf_op jit(solution)/shard_map/all_gather | solution.py:264
  103.1 6.3 %shard_map.110 = bf16[8,256,256]{2,1,0:T(8,128)(2,1)} custom-call(s32[1]{0:T(128)} %bitcast.3.scalars, f32[2]{0:T(128)S(1)} %multiply_power_fusion.slopes, bf16[256,2048]{1,0:T(8,128)(2,1)S(1)} %multiply_convert_fusion.normed, bf16[2048,2816]{1,0:T(8,128)(2,1)} %all-gather.3.cloned.1.call-done.weights.gathered, bf16[1024,256]{1,0:T(8,128)(2,1)S(1)} %bitcast.30, ...), custom_call_target="tpu_custom_call" | custom-call | tf_op jit(solution)/shard_map/pallas_call | solution.py:89
  109.4 0.0 all-to-all-done.2.near
  109.4 8.5 %collective-permute-start.1 = (bf16[8,16,64,256]{3,2,1,0:T(8,128)(2,1)}, bf16[8,16,64,256]{3,2,1,0:T(8,128)(2,1)}, u32[]{:S(2)}, u32[]{:S(2)}) collective-permute-start(bf16[8,16,64,256]{3,2,1,0:T(8,128)(2,1)} %all-to-all-done.2.near), channel_id=1, source_target_pairs={{0,1},{1,0},{2,3},{3,2},{4,5},{5,4},{6,7},{7,6},{8,9},{9,8},{10,11... | collective-permute-start | bytes 12582920 | tf_op jit(solution)/shard_map/ppermute | solution.py:17
  117.9 3.6 %all-to-all-start.1 = ((bf16[8,256,256]{2,1,0:T(8,128)(2,1)}), bf16[8,256,256]{2,1,0:T(8,128)(2,1)S(1)}, u32[]{:S(2)}, u32[]{:S(2)}) async-start(bf16[8,256,256]{2,1,0:T(8,128)(2,1)} %shard_map.110), calls=%async_computation.1 | async-start | bytes 2097152 | tf_op jit(solution)/shard_map/all_to_all | solution.py:233
  121.5 0.1 pad_add_fusion.place
  121.6 15.8 %all-to-all-done.1.attns = bf16[8,256,256]{2,1,0:T(8,128)(2,1)S(1)} async-done(((bf16[8,256,256]{2,1,0:T(8,128)(2,1)}), bf16[8,256,256]{2,1,0:T(8,128)(2,1)S(1)}, u32[]{:S(2)}, u32[]{:S(2)}) %all-to-all-start.1) | async-done | bytes 1048608 | tf_op jit(solution)/shard_map/all_to_all | solution.py:233
  137.3 0.0 collective-permute-done.1.far
  137.3 9.1 %shard_map.111 = (bf16[8,256,256]{2,1,0:T(8,128)(2,1)S(1)}, bf16[256,256]{1,0:T(8,128)(2,1)S(1)}) custom-call(s32[2]{0:T(128)S(1)} %pad_add_fusion.place, bf16[8,256,256]{2,1,0:T(8,128)(2,1)S(1)} %all-to-all-done.1.attns, bf16[8,256,256]{2,1,0:T(8,128)(2,1)S(1)} %all-to-all-done.tokens, f32[1,2048]{1,0:T(1,128)S(1)} %bitcast.31, ...), custom_call_target="tpu_custom_call" | custom-call | tf_op jit(solution)/shard_map/pallas_call | solution.py:168
  146.4 17.4 %all_to_all.20 = bf16[8,256,256]{2,1,0:T(8,128)(2,1)S(1)} all-to-all(bf16[8,256,256]{2,1,0:T(8,128)(2,1)S(1)} %get-tuple-element.20), channel_id=1, replica_groups=mesh['rep'=2,'row'=8,'z'=16,'core'=2] {'row'}, dimensions={0} | all-to-all | bytes 2097152 | tf_op jit(solution)/shard_map/all_to_all | solution.py:233
  163.8 0.1 convert_reduce_fusion.1
  164.0 0.7 fusion.2
  (19 shorter events, 0.1 us)
Async XLA Ops:
  6.5 59.7 %copy-start = (s32[2,1]{0,1:T(1,128)S(1)}, s32[2,1]{0,1:T(1,128)}, u32[]{:S(2)}) copy-start(s32[2,1]{0,1:T(1,128)} %param.20) | copy-start | bytes 28
  6.5 12.7 %copy-start.10 = (bf16[256,64]{0,1:T(8,128)(2,1)S(1)}, bf16[256,64]{0,1:T(8,128)(2,1)}, u32[]{:S(2)}) copy-start(bf16[256,64]{0,1:T(8,128)(2,1)} %param.13) | copy-start | bytes 98308
  6.5 96.6 %all-gather.3.cloned.1.call-start = ((), (), s32[]{:S(2)}) async-start(), calls=%async_computation.4 | async-start | bytes 11894784 | tf_op jit(solution)/shard_map/all_gather | solution.py:264
  9.5 47.9 %collective-permute-start = (bf16[1,2,8,128,256]{4,3,2,1,0:T(8,128)(2,1)}, bf16[1,2,8,128,256]{4,3,2,1,0:T(8,128)(2,1)S(1)}, u32[]{:S(2)}, u32[]{:S(2)}) collective-permute-start(bf16[1,2,8,128,256]{4,3,2,1,0:T(8,128)(2,1)} %param.18), channel_id=1, source_target_pairs={{0,256},{256,0},{1,257},{257,1},{2,258},{258,2},{3,259},{259,3},{4... | collective-permute-start | bytes 3145736 | tf_op jit(solution)/shard_map/ppermute | solution.py:17
  15.0 42.4 %all-to-all-start = ((bf16[8,256,256]{2,1,0:T(8,128)(2,1)}), bf16[8,256,256]{2,1,0:T(8,128)(2,1)S(1)}, u32[]{:S(2)}, u32[]{:S(2)}) async-start(bf16[8,256,256]{2,1,0:T(8,128)(2,1)} %get-tuple-element.13), calls=%async_computation | async-start | bytes 2097152 | tf_op jit(solution)/shard_map/all_to_all | solution.py:233
  57.4 1.0 copy-start.8
  60.9 6.0 %copy-start.12 = (s32[2,1,8]{2,1,0:T(1,128)S(1)}, s32[2,1,8]{2,1,0:T(1,128)}, u32[]{:S(2)}) copy-start(s32[2,1,8]{2,1,0:T(1,128)} %param.19) | copy-start | bytes 196
  60.9 6.0 %copy-start.7 = (bf16[1,2,8,128,256]{4,3,2,1,0:T(8,128)(2,1)S(1)}, bf16[1,2,8,128,256]{4,3,2,1,0:T(8,128)(2,1)}, u32[]{:S(2)}) copy-start(bf16[1,2,8,128,256]{4,3,2,1,0:T(8,128)(2,1)} %param.18) | copy-start | bytes 3145732
  60.9 48.6 %all-to-all-start.2 = ((bf16[8,16,64,256]{3,2,1,0:T(8,128)(2,1)}), bf16[8,16,64,256]{3,2,1,0:T(8,128)(2,1)}, u32[]{:S(2)}, u32[]{:S(2)}) async-start(bf16[8,16,64,256]{3,2,1,0:T(8,128)(2,1)} %broadcast_in_dim.2), calls=%async_computation.2 | async-start | bytes 8388608 | tf_op jit(solution)/shard_map/all_to_all | solution.py:233
  67.0 2.8 %copy-start.9 = (bf16[1,2,8,128,256]{4,3,2,1,0:T(8,128)(2,1)S(1)}, bf16[1,2,8,128,256]{4,3,2,1,0:T(8,128)(2,1)}, u32[]{:S(2)}) copy-start(bf16[1,2,8,128,256]{4,3,2,1,0:T(8,128)(2,1)} %copy-done.8) | copy-start | bytes 3145732
  78.0 1.1 copy-start.3
  78.0 1.2 copy-start.4
  78.0 1.4 copy-start.5
  78.0 1.5 copy-start.6
  78.3 2.1 %copy-start.2 = (f32[256,2048]{1,0:T(8,128)S(1)}, f32[256,2048]{1,0:T(8,128)}, u32[]{:S(2)}) copy-start(f32[256,2048]{1,0:T(8,128)} %copy.13) | copy-start | bytes 6291460
  78.3 2.1 %copy-start.11 = (f32[2048]{0:T(1024)S(1)}, f32[2048]{0:T(1024)}, u32[]{:S(2)}) copy-start(f32[2048]{0:T(1024)} %param.16) | copy-start | bytes 24580
  109.4 27.9 %copy-start.1 = (f32[2048]{0:T(1024)S(1)}, f32[2048]{0:T(1024)}, u32[]{:S(2)}) copy-start(f32[2048]{0:T(1024)} %param.17) | copy-start | bytes 24580
  109.4 27.9 %collective-permute-start.1 = (bf16[8,16,64,256]{3,2,1,0:T(8,128)(2,1)}, bf16[8,16,64,256]{3,2,1,0:T(8,128)(2,1)}, u32[]{:S(2)}, u32[]{:S(2)}) collective-permute-start(bf16[8,16,64,256]{3,2,1,0:T(8,128)(2,1)} %all-to-all-done.2.near), channel_id=1, source_target_pairs={{0,1},{1,0},{2,3},{3,2},{4,5},{5,4},{6,7},{7,6},{8,9},{9,8},{10,11... | collective-permute-start | bytes 12582920 | tf_op jit(solution)/shard_map/ppermute | solution.py:17
  117.9 19.4 %all-to-all-start.1 = ((bf16[8,256,256]{2,1,0:T(8,128)(2,1)}), bf16[8,256,256]{2,1,0:T(8,128)(2,1)S(1)}, u32[]{:S(2)}, u32[]{:S(2)}) async-start(bf16[8,256,256]{2,1,0:T(8,128)(2,1)} %shard_map.110), calls=%async_computation.1 | async-start | bytes 2097152 | tf_op jit(solution)/shard_map/all_to_all | solution.py:233
Sparse Core Ops, SparseCore 0:
  9.6 93.4 all-gather.2

commit v6 on v5

--- a/solution.py
+++ b/solution.py
@@ -24,7 +24,7 @@
     return centred * lax.rsqrt(spread + 1e-05) * gain
 
 
-def attend_kernel(scalars, slopes, normed, weights, keys, values, copies, total, attn):
+def attend_kernel(scalars, slopes, normed, weights, keys, values, _, copies, total, attn):
     step = pl.program_id(0)
     product = jnp.dot(normed[...], weights[...], preferred_element_type=jnp.float32)
 
@@ -81,7 +81,7 @@
             copies[row] = attn[...]
 
 
-def attend(normed, weights, keys, values, length, slopes, rows):
+def attend(normed, weights, keys, values, arrived, length, slopes, rows):
     seq, width = normed.shape
     share = keys.shape[1]
     steps = 2
@@ -97,6 +97,7 @@
                 pl.BlockSpec((deep, 3 * share), lambda k, *_: (k, 0)),
                 pl.BlockSpec(keys.shape, lambda k, *_: (0, 0)),
                 pl.BlockSpec(values.shape, lambda k, *_: (0, 0)),
+                pl.BlockSpec(memory_space=pl.ANY),
             ],
             out_specs=pl.BlockSpec((rows, seq, share), lambda k, *_: (0, 0, 0)),
             scratch_shapes=[
@@ -105,7 +106,7 @@
             ],
         ),
         compiler_params=pltpu.CompilerParams(vmem_limit_bytes=48 << 20),
-    )(length.reshape(1), slopes, normed, weights, keys, values)
+    )(length.reshape(1), slopes, normed, weights, keys, values, arrived)
 
 
 def feed_kernel(place, attns, tokens, gain, near, far, gathered, down, state_local,
@@ -264,7 +265,8 @@
     weights = lax.all_gather(shard, ("z", "core"), axis=0, tiled=True)
     other = swapped(kv_pool, "rep", 0)
     out_block = lax.all_gather(w_out.T, "z", axis=0, tiled=False)
-    out_block, spread_tokens, other = lax.optimization_barrier((out_block, spread_tokens, other))
+    arrived = other[0, 0, 0, :16, :128]
+    out_block, spread_tokens, arrived = lax.optimization_barrier((out_block, spread_tokens, arrived))
     near = row_gather(out_block)
     rows = jnp.swapaxes(spread_tokens, 0, 1).reshape(seq, D)
     normed = normalize(rows.astype(jnp.float32), ln1_gain).astype(jnp.bfloat16)
@@ -281,7 +283,7 @@
     cache_keys = jnp.where(flag, pages_of(other[0, 0], table), pages_of(kv_pool[0, 0], table))
     cache_values = jnp.where(flag, pages_of(other[0, 1], table), pages_of(kv_pool[0, 1], table))
     attn_copies = attend(
-        normed, weights, cache_keys, cache_values, length, slopes, lax.axis_size("row")
+        normed, weights, cache_keys, cache_values, arrived, length, slopes, lax.axis_size("row")
     )
     attns = row_exchange(attn_copies)
     near, _ = lax.optimization_barrier((near, attn_copies))

time: 173 us -> 172 us (level)
  transfers between devices with their start and end apart: 6 -> 6, of which waited for: 2 -> 2; matrix products, arithmetic and copies ran while one was open for 9% -> 10% of each run, Pallas kernels for 4% -> 4%
where the time goes in v6:
time: 172 us; the launch traced here: 170 us
  blocking collectives  55.5 us (32%)
  waiting for transfers between devices  37.9 us (22%)
  starting transfers between devices  25.4 us (15%)
  Pallas kernels  18.4 us (11%)
  local copies, waits for them, and re-layouts  15.4 us (9%)
  between operations  14.2 us (8%)
  other arithmetic  3.6 us (2%)
    all_gather x1, blocking collectives, local(): out_block = lax.all_gather(w_out.T, 'z', axis=0, tiled=False)  38.1 us
    all_gather x1, waiting for transfers between devices, local(): weights = lax.all_gather(shard, ('z', 'core'), axis=0, tiled=True)  22.1 us
    all_to_all x1, blocking collectives, row_exchange(): return lax.all_to_all(parts, 'row', 0, 0, tiled=True)  17.4 us
    all_to_all x3, waiting for transfers between devices, row_exchange(): return lax.all_to_all(parts, 'row', 0, 0, tiled=True)  15.8 us
    ppermute x2, starting transfers between devices, swapped(): lax.ppermute(value, axis, [(i, i ^ 1 << apart) for i in range(lax.axis_si...  12.9 us
    all_to_all x3, starting transfers between devices, row_exchange(): return lax.all_to_all(parts, 'row', 0, 0, tiled=True)  12.5 us
    pallas_call x1, Pallas kernels, feed(): pl.pallas_call(feed_kernel, out_shape=(jax.ShapeDtypeStruct(attns.shape,...  9.08 us
    pallas_call x1, Pallas kernels, attend(): pl.pallas_call(attend_kernel, out_shape=jax.ShapeDtypeStruct((rows, seq,...  6.38 us
  transfers between devices with their start and end apart: 6, of which 2 were waited for; matrix products, arithmetic and copies ran while one was open for 10% of the time, Pallas kernels for 4%

profile of v6, /device:TPU:1, one launch (start us, length us, event | category | flops | bytes accessed | tf_op | source)
XLA Modules:
  0.0 170.5 jit_solution(421138248539176818)
XLA Ops:
  6.5 0.0 copy-start
  6.5 0.0 all-gather.3.cloned.1.call-start
  6.5 2.9 %shard_map.109 = (bf16[64,2816]{1,0:T(8,128)(2,1)}, bf16[8,256,256]{2,1,0:T(8,128)(2,1)}) custom-call(bf16[3,64,256]{2,1,0:T(8,128)(2,1)} %bitcast.38, bf16[64,1024]{1,0:T(8,128)(2,1)} %up.1, bf16[64,1024]{1,0:T(8,128)(2,1)} %bitcast.36, bf16[256,256]{1,0:T(8,128)(2,1)} %bitcast.37), custom_call_target="tpu_custom_call" | custom-call | tf_op jit(solution)/shard_map/pallas_call | solution.py:221
  9.4 0.0 all-gather.3.cloned.1.call-update
  9.5 5.5 %collective-permute-start = (bf16[1,2,8,128,256]{4,3,2,1,0:T(8,128)(2,1)}, bf16[1,2,8,128,256]{4,3,2,1,0:T(8,128)(2,1)S(1)}, u32[]{:S(2)}, u32[]{:S(2)}) collective-permute-start(bf16[1,2,8,128,256]{4,3,2,1,0:T(8,128)(2,1)} %param.18), channel_id=1, source_target_pairs={{0,256},{256,0},{1,257},{257,1},{2,258},{258,2},{3,259},{259,3},{4... | collective-permute-start | bytes 3145736 | tf_op jit(solution)/shard_map/ppermute | solution.py:17
  15.0 4.2 %all-to-all-start = ((bf16[8,256,256]{2,1,0:T(8,128)(2,1)}), bf16[8,256,256]{2,1,0:T(8,128)(2,1)S(1)}, u32[]{:S(2)}, u32[]{:S(2)}) async-start(bf16[8,256,256]{2,1,0:T(8,128)(2,1)} %get-tuple-element.13), calls=%async_computation | async-start | bytes 2097152 | tf_op jit(solution)/shard_map/all_to_all | solution.py:234
  19.2 0.0 copy-done.7
  19.2 38.1 %all-gather = bf16[1024,256]{1,0:T(8,128)(2,1)S(1)} all-gather(bf16[64,256]{1,0:T(8,128)(2,1)S(1)} %bitcast.39), channel_id=2, replica_groups=mesh['rep'=2,'row'=8,'z'=16,'core'=2] {'z'}, dimensions={0}, use_global_device_ids=true | all-gather | bytes 557056 | tf_op jit(solution)/shard_map/all_gather | solution.py:267
  57.3 0.0 collective-permute-done
  57.3 0.0 all-to-all-done.tokens
  57.4 2.5 %broadcast_in_dim.2 = bf16[8,16,64,256]{3,2,1,0:T(8,128)(2,1)} broadcast(bf16[16,64,256]{2,1,0:T(8,128)(2,1)S(1)} %bitcast.35), dimensions={1,2,3} | broadcast | bytes 4718592 | tf_op jit(solution)/shard_map/broadcast_in_dim | solution.py:238
  59.8 4.7 %all-to-all-start.2 = ((bf16[8,16,64,256]{3,2,1,0:T(8,128)(2,1)}), bf16[8,16,64,256]{3,2,1,0:T(8,128)(2,1)}, u32[]{:S(2)}, u32[]{:S(2)}) async-start(bf16[8,16,64,256]{3,2,1,0:T(8,128)(2,1)} %broadcast_in_dim.2), calls=%async_computation.2 | async-start | bytes 8388608 | tf_op jit(solution)/shard_map/all_to_all | solution.py:234
  65.2 0.0 copy-done
  65.2 0.7 constant_dynamic-slice_fusion
  65.9 0.0 copy-done.9
  65.9 1.3 slice_bitcast_fusion.2
  67.2 1.4 gather_fusion.3
  68.6 1.4 gather_fusion.1
  69.9 0.1 slice_bitcast_fusion
  70.0 1.4 gather_fusion.2
  71.4 1.4 gather_fusion
  72.8 1.5 convert_bitcast_fusion
  74.4 1.9 %copy.12 = f32[256,8,256]{0,2,1:T(8,128)S(1)} copy(f32[256,8,256]{2,0,1:T(8,128)} %convert_bitcast_fusion) | data formatting | bytes 4194304 | tf_op jit(solution)/shard_map/convert_element_type | solution.py:272
  76.3 1.9 %copy.13 = f32[256,2048]{1,0:T(8,128)} copy(f32[256,2048]{0,1:T(8,128)S(1)} %bitcast.34) | data formatting | bytes 4194304 | tf_op jit(solution)/shard_map/convert_element_type | solution.py:272
  78.2 0.2 convert_reduce_fusion
  78.4 0.0 copy-start.8
  78.4 0.4 fusion.1
  78.9 0.4 copy-done.3
  79.2 0.2 copy-done.4
  79.4 0.2 copy-done.5
  79.5 0.2 copy-done.6
  79.7 0.1 broadcast_select_fusion
  79.8 0.7 copy-done.2
  80.5 0.0 copy-done.8
  80.5 0.4 multiply_convert_fusion.normed
  80.9 22.1 %all-gather.3.cloned.1.call-done.weights.gathered = bf16[2048,2816]{1,0:T(8,128)(2,1)} async-done(((bf16[64,2816]{1,0:T(8,128)(2,1)}), bf16[2048,2816]{1,0:T(8,128)(2,1)}) %all-gather.3.cloned.1.call-update) | async-done | bytes 11534352 | tf_op jit(solution)/shard_map/all_gather | solution.py:265
  103.1 6.4 %shard_map.110 = bf16[8,256,256]{2,1,0:T(8,128)(2,1)} custom-call(s32[1]{0:T(128)} %bitcast.3.scalars, f32[2]{0:T(128)S(1)} %multiply_power_fusion.slopes, bf16[256,2048]{1,0:T(8,128)(2,1)S(1)} %multiply_convert_fusion.normed, bf16[2048,2816]{1,0:T(8,128)(2,1)} %all-gather.3.cloned.1.call-done.weights.gathered, bf16[1024,256]{1,0:T(8,128)(2,1)S(1)} %bitcast.32, ...), custom_call_target="tpu_custom_call" | custom-call | tf_op jit(solution)/shard_map/pallas_call | solution.py:89
  109.4 0.0 all-to-all-done.2.near
  109.5 7.4 %collective-permute-start.1 = (bf16[8,16,64,256]{3,2,1,0:T(8,128)(2,1)}, bf16[8,16,64,256]{3,2,1,0:T(8,128)(2,1)}, u32[]{:S(2)}, u32[]{:S(2)}) collective-permute-start(bf16[8,16,64,256]{3,2,1,0:T(8,128)(2,1)} %all-to-all-done.2.near), channel_id=1, source_target_pairs={{0,1},{1,0},{2,3},{3,2},{4,5},{5,4},{6,7},{7,6},{8,9},{9,8},{10,11... | collective-permute-start | bytes 12582920 | tf_op jit(solution)/shard_map/ppermute | solution.py:17
  116.9 3.6 %all-to-all-start.1 = ((bf16[8,256,256]{2,1,0:T(8,128)(2,1)}), bf16[8,256,256]{2,1,0:T(8,128)(2,1)S(1)}, u32[]{:S(2)}, u32[]{:S(2)}) async-start(bf16[8,256,256]{2,1,0:T(8,128)(2,1)} %shard_map.110), calls=%async_computation.1 | async-start | bytes 2097152 | tf_op jit(solution)/shard_map/all_to_all | solution.py:234
  120.5 0.1 pad_add_fusion.place
  120.5 15.8 %all-to-all-done.1.attns = bf16[8,256,256]{2,1,0:T(8,128)(2,1)S(1)} async-done(((bf16[8,256,256]{2,1,0:T(8,128)(2,1)}), bf16[8,256,256]{2,1,0:T(8,128)(2,1)S(1)}, u32[]{:S(2)}, u32[]{:S(2)}) %all-to-all-start.1) | async-done | bytes 1048608 | tf_op jit(solution)/shard_map/all_to_all | solution.py:234
  136.3 0.0 collective-permute-done.1.far
  136.3 0.0 copy-done.1
  136.3 9.1 %shard_map.111 = (bf16[8,256,256]{2,1,0:T(8,128)(2,1)S(1)}, bf16[256,256]{1,0:T(8,128)(2,1)S(1)}) custom-call(s32[2]{0:T(128)S(1)} %pad_add_fusion.place, bf16[8,256,256]{2,1,0:T(8,128)(2,1)S(1)} %all-to-all-done.1.attns, bf16[8,256,256]{2,1,0:T(8,128)(2,1)S(1)} %all-to-all-done.tokens, f32[1,2048]{1,0:T(1,128)S(1)} %bitcast.33, ...), custom_call_target="tpu_custom_call" | custom-call | tf_op jit(solution)/shard_map/pallas_call | solution.py:169
  145.4 17.4 %all_to_all.20 = bf16[8,256,256]{2,1,0:T(8,128)(2,1)S(1)} all-to-all(bf16[8,256,256]{2,1,0:T(8,128)(2,1)S(1)} %get-tuple-element.20), channel_id=1, replica_groups=mesh['rep'=2,'row'=8,'z'=16,'core'=2] {'row'}, dimensions={0} | all-to-all | bytes 2097152 | tf_op jit(solution)/shard_map/all_to_all | solution.py:234
  162.8 0.1 convert_reduce_fusion.1
  162.9 0.7 fusion.2
  (14 shorter events, 0.0 us)
Async XLA Ops:
  6.5 58.7 %copy-start = (s32[2,1]{0,1:T(1,128)S(1)}, s32[2,1]{0,1:T(1,128)}, u32[]{:S(2)}) copy-start(s32[2,1]{0,1:T(1,128)} %param.20) | copy-start | bytes 28
  6.5 12.7 %copy-start.7 = (bf16[256,64]{0,1:T(8,128)(2,1)S(1)}, bf16[256,64]{0,1:T(8,128)(2,1)}, u32[]{:S(2)}) copy-start(bf16[256,64]{0,1:T(8,128)(2,1)} %param.13) | copy-start | bytes 98308
  6.5 96.5 %all-gather.3.cloned.1.call-start = ((), (), s32[]{:S(2)}) async-start(), calls=%async_computation.4 | async-start | bytes 11894784 | tf_op jit(solution)/shard_map/all_gather | solution.py:265
  9.5 47.9 %collective-permute-start = (bf16[1,2,8,128,256]{4,3,2,1,0:T(8,128)(2,1)}, bf16[1,2,8,128,256]{4,3,2,1,0:T(8,128)(2,1)S(1)}, u32[]{:S(2)}, u32[]{:S(2)}) collective-permute-start(bf16[1,2,8,128,256]{4,3,2,1,0:T(8,128)(2,1)} %param.18), channel_id=1, source_target_pairs={{0,256},{256,0},{1,257},{257,1},{2,258},{258,2},{3,259},{259,3},{4... | collective-permute-start | bytes 3145736 | tf_op jit(solution)/shard_map/ppermute | solution.py:17
  15.0 42.4 %all-to-all-start = ((bf16[8,256,256]{2,1,0:T(8,128)(2,1)}), bf16[8,256,256]{2,1,0:T(8,128)(2,1)S(1)}, u32[]{:S(2)}, u32[]{:S(2)}) async-start(bf16[8,256,256]{2,1,0:T(8,128)(2,1)} %get-tuple-element.13), calls=%async_computation | async-start | bytes 2097152 | tf_op jit(solution)/shard_map/all_to_all | solution.py:234
  59.8 6.0 %copy-start.9 = (s32[2,1,8]{2,1,0:T(1,128)S(1)}, s32[2,1,8]{2,1,0:T(1,128)}, u32[]{:S(2)}) copy-start(s32[2,1,8]{2,1,0:T(1,128)} %param.19) | copy-start | bytes 196
  59.8 49.6 %all-to-all-start.2 = ((bf16[8,16,64,256]{3,2,1,0:T(8,128)(2,1)}), bf16[8,16,64,256]{3,2,1,0:T(8,128)(2,1)}, u32[]{:S(2)}, u32[]{:S(2)}) async-start(bf16[8,16,64,256]{3,2,1,0:T(8,128)(2,1)} %broadcast_in_dim.2), calls=%async_computation.2 | async-start | bytes 8388608 | tf_op jit(solution)/shard_map/all_to_all | solution.py:234
  78.2 1.0 copy-start.3
  78.2 1.2 copy-start.4
  78.2 1.4 copy-start.5
  78.2 1.5 copy-start.6
  78.4 2.1 %copy-start.2 = (f32[256,2048]{1,0:T(8,128)S(1)}, f32[256,2048]{1,0:T(8,128)}, u32[]{:S(2)}) copy-start(f32[256,2048]{1,0:T(8,128)} %copy.13) | copy-start | bytes 6291460
  78.4 2.1 %copy-start.8 = (f32[2048]{0:T(1024)S(1)}, f32[2048]{0:T(1024)}, u32[]{:S(2)}) copy-start(f32[2048]{0:T(1024)} %param.16) | copy-start | bytes 24580
  109.4 26.8 %copy-start.1 = (f32[2048]{0:T(1024)S(1)}, f32[2048]{0:T(1024)}, u32[]{:S(2)}) copy-start(f32[2048]{0:T(1024)} %param.17) | copy-start | bytes 24580
  109.5 26.8 %collective-permute-start.1 = (bf16[8,16,64,256]{3,2,1,0:T(8,128)(2,1)}, bf16[8,16,64,256]{3,2,1,0:T(8,128)(2,1)}, u32[]{:S(2)}, u32[]{:S(2)}) collective-permute-start(bf16[8,16,64,256]{3,2,1,0:T(8,128)(2,1)} %all-to-all-done.2.near), channel_id=1, source_target_pairs={{0,1},{1,0},{2,3},{3,2},{4,5},{5,4},{6,7},{7,6},{8,9},{9,8},{10,11... | collective-permute-start | bytes 12582920 | tf_op jit(solution)/shard_map/ppermute | solution.py:17
  116.9 19.4 %all-to-all-start.1 = ((bf16[8,256,256]{2,1,0:T(8,128)(2,1)}), bf16[8,256,256]{2,1,0:T(8,128)(2,1)S(1)}, u32[]{:S(2)}, u32[]{:S(2)}) async-start(bf16[8,256,256]{2,1,0:T(8,128)(2,1)} %shard_map.110), calls=%async_computation.1 | async-start | bytes 2097152 | tf_op jit(solution)/shard_map/all_to_all | solution.py:234
Sparse Core Ops, SparseCore 0:
  9.6 93.4 all-gather.2
